TPU v7x, 128 devices: a whole 4x4x4 slice. The times are simulated.
128 devices in a mesh: tm: 32 (over z, x, core), word: 4 (over y).
Axes of the slice: x: 4, y: 4, z: 4, core: 2. Of those that a mesh axis runs over, the one named last changes fastest.
Arguments:
- pseudo_obs: float32 [64, 100, 10240], P('tm', None, 'word'), may hold values from -12 to 12
- filter_decay: float32 [64, 100], P('tm'), may hold values from 0.45 to 1
- smooth_gain: float32 [64, 100], P('tm'), may hold values from 0.45 to 1
- log_norm: float32 [64, 100], P('tm'), may hold values from 8.7 to 9.9
- doc_weights: bfloat16 [64, 100, 512], P('tm'), may hold values from 0.0009994507 to 0.099609375
- doc_ids: int32 [64, 65536], P('tm', 'word'), may hold values from 0 to 511
- word_ids: int32 [64, 65536], P('tm', 'word'), may hold values from 0 to 10239, as said below
- counts: int32 [64, 65536], P('tm', 'word'), may hold values from 1 to 11, as said below
Outputs:
- grad_obs: float32 [64, 100, 10240], P('tm', None, 'word')
- topic_counts: float32 [64, 100, 512], P('tm', None, 'word')
Inputs may be any that keep to these rules, and one draw needn't show every extreme that they name: `word_ids`: entry e of a slice names a word from (e // 16384) * 2560 to (e // 16384 + 1) * 2560 - 1; a slice may repeat a document and word, and their counts add. `counts`: the count of entry e lies from 1 to 2 + 3 * (e // 16384).
All inputs are finite; a program needn't handle non-finite values.
Results may differ from a plain program's by a relative error of at most 0.00066.
Values sent between devices are 32-bit elements; how exact they have to be, the bound alone decides.
A program may use at most 192 MiB of HBM per device.

v0:
```python
import jax
import jax.numpy as jnp
from jax import lax
from jax.sharding import PartitionSpec as P


def carried_in(value, axis, join, neutral, backward):
    count, mine = (lax.axis_size(axis), lax.axis_index(axis))
    pieces = jax.tree.map(lambda part: lax.all_gather(part, axis), value)
    if backward:
        pieces = jax.tree.map(lambda part: part[::-1], pieces)
        mine = count - 1 - mine
    running = jax.tree.map(
        lambda part, zero: jnp.full_like(part, 0) + jnp.asarray(zero, part.dtype), value, neutral
    )

    def lap(position, running):
        longer = join(running, jax.tree.map(lambda part: part[position], pieces))
        return jax.tree.map(lambda new, old: jnp.where(position < mine, new, old), longer, running)

    return lax.fori_loop(0, count - 1, lap, running)


def combine_affine(earlier, later):
    return (earlier[0] * later[0], later[0][:, None] * earlier[1] + later[1])


def final_keep(gains, positions, length_all):
    return jnp.where((positions == length_all - 1)[:, None], 1.0, 1.0 - gains)


def local_chain(factors, added, incoming, reverse):

    def advance(current, element):
        factor_row, added_row = element
        updated = factor_row[:, None] * current + added_row
        return (updated, (updated, current))

    last_state, outputs = lax.scan(advance, incoming, (factors, added), reverse=reverse)
    return (last_state, outputs[0], outputs[1])


def chain_scan(factors, added, reverse, exclusive):
    zero_state = jnp.zeros(added.shape[1:], jnp.float32)
    last_state, inclusive, previous = local_chain(factors, added, zero_state, reverse)
    whole_factor = jnp.prod(factors, axis=0)
    identity = (jnp.ones_like(whole_factor), zero_state)
    if reverse:
        carried = carried_in((whole_factor, last_state), "tm", combine_affine, identity, True)
        through = jnp.cumprod(factors[::-1], axis=0)[::-1]
        before = jnp.concatenate([through[1:], jnp.ones_like(through[:1])], axis=0)
    else:
        carried = carried_in((whole_factor, last_state), "tm", combine_affine, identity, False)
        through = jnp.cumprod(factors, axis=0)
        before = jnp.concatenate([jnp.ones_like(through[:1]), through[:-1]], axis=0)
    entering = carried[1]
    if exclusive:
        return previous + before[:, :, None] * entering[None]
    return inclusive + through[:, :, None] * entering[None]


def local(pseudo_obs, filter_decay, smooth_gain, log_norm, doc_weights, doc_ids, word_ids, counts):
    slices_dev = pseudo_obs.shape[0]
    positions = lax.axis_index("tm") * slices_dev + jnp.arange(slices_dev, dtype=jnp.int32)
    keep_share = final_keep(smooth_gain, positions, slices_dev * lax.axis_size("tm"))
    filtered = chain_scan(filter_decay, (1.0 - filter_decay)[:, :, None] * pseudo_obs, False, False)
    smoothed = chain_scan(smooth_gain, keep_share[:, :, None] * filtered, True, False)
    vocab_dev = pseudo_obs.shape[2]
    word_base = lax.axis_index("word") * vocab_dev

    def slice_terms(inputs):
        smooth_row, norm_row, weight_row, doc_rows, word_cols, count_vals = inputs
        doc_count = weight_row.shape[1]
        topic_word = jnp.exp(smooth_row - norm_row[:, None])
        topic_round = lax.optimization_barrier(topic_word.astype(jnp.bfloat16))
        flat_index = doc_rows * vocab_dev + (word_cols - word_base)
        flat_counts = (
            jnp.zeros((doc_count * vocab_dev,), jnp.float32)
            .at[flat_index]
            .add(count_vals.astype(jnp.float32))
        )
        dense_counts = flat_counts.reshape(doc_count, vocab_dev)
        mixture = lax.dot_general(
            weight_row, topic_round, (((0,), (0,)), ((), ())), preferred_element_type=jnp.float32
        )
        count_ratio = (dense_counts / mixture).astype(jnp.bfloat16)
        topic_sums = lax.dot_general(
            topic_round, count_ratio, (((1,), (1,)), ((), ())), preferred_element_type=jnp.float32
        )
        weighted = jnp.dot(weight_row, count_ratio, preferred_element_type=jnp.float32)
        expected = topic_round.astype(jnp.float32) * weighted
        return (topic_sums, expected, topic_word)

    topic_sums, expected, topic_word = lax.map(
        slice_terms, (smoothed, log_norm, doc_weights, doc_ids, word_ids, counts)
    )
    totals = lax.psum(jnp.sum(expected, axis=2), "word")
    own_sums = lax.psum_scatter(topic_sums, "word", scatter_dimension=2, tiled=True)
    share_len = own_sums.shape[2]
    own_weights = lax.dynamic_slice_in_dim(
        doc_weights, lax.axis_index("word") * share_len, share_len, 2
    )
    topic_counts = own_weights.astype(jnp.float32) * own_sums
    word_grad = expected - totals[:, :, None] * topic_word
    smooth_prev = chain_scan(smooth_gain, smooth_gain[:, :, None] * word_grad, False, True)
    hidden = keep_share[:, :, None] * (word_grad + smooth_prev)
    filter_next = chain_scan(filter_decay, filter_decay[:, :, None] * hidden, True, True)
    grad_obs = (1.0 - filter_decay)[:, :, None] * (hidden + filter_next)
    return (grad_obs, topic_counts)


def solution(mesh):
    return jax.shard_map(
        local,
        mesh=mesh,
        in_specs=(
            P("tm", None, "word"),
            P("tm", None),
            P("tm", None),
            P("tm", None),
            P("tm", None, None),
            P("tm", "word"),
            P("tm", "word"),
            P("tm", "word"),
        ),
        out_specs=(P("tm", None, "word"), P("tm", None, "word")),
        check_vma=False,
    )
```

profile of v0, /device:TPU:1, one launch (start us, length us, event | category | flops | bytes accessed | tf_op | source)
XLA Modules:
  0.0 1154.2 jit_solution(10494142934381497400)
XLA Ops:
  13.7 38.4 %while.131 = (s32[]{:T(128)}, f32[100,2560]{1,0:T(8,128)S(1)}, f32[2,100,2560]{2,0,1:T(2,128)}, f32[2,100]{1,0:T(2,128)S(1)}, f32[2,100,2560]{2,0,1:T(2,128)}, /*index=5*/s32[]{:T(128)}, s32[]{:T(128)}) while((s32[]{:T(128)}, f32[100,2560]{1,0:T(8,128)S(1)}, f32[2,100,2560]{2,0,1:T(2,128)}, f32[2,100]{1,0:T(2,128)S(1)}, ...), condition=%wide.region_1.2_spmd.clone, body=%wide.region_0.1_spmd.clone.sunk | while | flops 768003 | bytes 9217299 | solution.py:39
  17.4 15.4 %dynamic_update_slice.52 = f32[2,100,2560]{2,0,1:T(2,128)} dynamic-update-slice(f32[2,100,2560]{2,0,1:T(2,128)} %get-tuple-element.1396, f32[1,100,2560]{2,0,1:T(1,128)S(1)} %copy.107, s32[]{:T(128)} %get-tuple-element.1394, s32[]{:T(128)} %constant.233.clone.1..sunk.1, s32[]{:T(128)} %constant.233.clone.1..sunk.1) | dynamic-update-slice | bytes 2048004 | tf_op jit(solution)/shard_map/while/body/jit(dynamic_update_index_in_dim)/dynamic_update_slice | solution.py:39
  36.6 15.4 %dynamic_update_slice.52 = f32[2,100,2560]{2,0,1:T(2,128)} dynamic-update-slice(f32[2,100,2560]{2,0,1:T(2,128)} %get-tuple-element.1396, f32[1,100,2560]{2,0,1:T(1,128)S(1)} %copy.107, s32[]{:T(128)} %get-tuple-element.1394, s32[]{:T(128)} %constant.233.clone.1..sunk.1, s32[]{:T(128)} %constant.233.clone.1..sunk.1) | dynamic-update-slice | bytes 2048004 | tf_op jit(solution)/shard_map/while/body/jit(dynamic_update_index_in_dim)/dynamic_update_slice | solution.py:39
  54.9 127.5 %all-reduce.3 = (f32[3200]{0:T(1024)S(1)}, f32[3200]{0:T(1024)S(1)}) all-reduce(f32[3200]{0:T(1024)S(1)} %dynamic-update-slice, f32[3200]{0:T(1024)S(1)} %dynamic-update-slice.1), channel_id=2, replica_groups=mesh['tm'=32,'word'=4] {'tm'}, use_global_device_ids=true, to_apply=%add.1 | all-reduce | flops 6400 | bytes 51200
  182.8 50.1 %while.132 = (s32[]{:T(128)}, f32[100,2560]{1,0:T(8,128)S(1)}, s32[]{:T(128)}, f32[32,100]{1,0:T(8,128)S(1)}, f32[32,100,2560]{2,1,0:T(8,128)}, /*index=5*/s32[]{:T(128)}, s32[]{:T(128)}) while((s32[]{:T(128)}, f32[100,2560]{1,0:T(8,128)S(1)}, s32[]{:T(128)}, f32[32,100]{1,0:T(8,128)S(1)}, f32[32,100,2560]{2,1,0:T(8,128)}, ...), condition=%wide.region_5.6_spmd.clone, body=%wide.region_4.5_spmd.clone.sunk | while | flops 1024004 | bytes 3073305 | solution.py:21
  249.1 115.1 %all-gather.17.cloned.1.call-done = f32[32,100,2560]{2,1,0:T(8,128)} async-done(((f32[1,100,2560]{2,1,0:T(8,128)}), f32[32,100,2560]{2,1,0:T(8,128)}) %all-gather.17.cloned.1.call-update) | async-done | bytes 32768016 | tf_op jit(solution)/shard_map/all_gather | solution.py:9
  364.2 22.8 %reverse.1 = f32[32,100,2560]{2,1,0:T(8,128)} reverse(f32[32,100,2560]{2,1,0:T(8,128)} %all-gather.17.cloned.1.call-done), dimensions={0} | reverse | bytes 65536000 | tf_op jit(solution)/shard_map/rev | solution.py:11
  387.0 50.1 %while.134 = (s32[]{:T(128)}, f32[100,2560]{1,0:T(8,128)S(1)}, s32[]{:T(128)}, f32[32,100]{1,0:T(8,128)S(1)}, f32[32,100,2560]{2,1,0:T(8,128)}, /*index=5*/s32[]{:T(128)}, s32[]{:T(128)}) while((s32[]{:T(128)}, f32[100,2560]{1,0:T(8,128)S(1)}, s32[]{:T(128)}, f32[32,100]{1,0:T(8,128)S(1)}, f32[32,100,2560]{2,1,0:T(8,128)}, ...), condition=%wide.region_11.12_spmd.clone, body=%wide.region_10.11_spmd.clone.sunk | while | flops 1024004 | bytes 3073305 | solution.py:21
  442.4 240.7 %while.130 = (s32[]{:T(128)}, f32[2,100,512]{2,1,0:T(8,128)}, f32[2,100,2560]{2,1,0:T(8,128)}, f32[2,100,2560]{2,0,1:T(2,128)}, f32[2,100,2560]{2,1,0:T(8,128)S(...) while((s32[]{:T(128)}, f32[2,100,512]{2,1,0:T(8,128)}, ...), condition=%wide.region_14.15_spmd, body=%wide.region_12.14_spmd.sunk | while | flops 790464512 | bytes 59595612 | solution.py:94
  444.7 88.4 %scatter_custom_fusion.5 = f32[1310720]{0:T(1024)} fusion(s32[16384]{0:T(1024)S(1)} %bitcast.160, f32[16384]{0:T(1024)S(1)} %bitcast.161, f32[]{:T(128)} %constant.234.clone.1..sunk), kind=kCustom, calls=%fused_computation.5.clone.1 | custom fusion | flops 16384 | bytes 5242884 | tf_op jit(solution)/shard_map/while/body/eval_jaxpr/scatter-add | solution.py:80
  547.4 15.4 %dynamic_update_slice.51 = f32[2,100,2560]{2,0,1:T(2,128)} dynamic-update-slice(f32[2,100,2560]{2,0,1:T(2,128)} %get-tuple-element.1488, f32[1,100,2560]{2,0,1:T(1,128)S(1)} %copy.105, s32[]{:T(128)} %get-tuple-element.1485, s32[]{:T(128)} %constant.233.clone.1..sunk, s32[]{:T(128)} %constant.233.clone.1..sunk) | dynamic-update-slice | bytes 2048004 | tf_op jit(solution)/shard_map/while/body/jit(dynamic_update_index_in_dim)/dynamic_update_slice | solution.py:39
  565.1 88.4 %scatter_custom_fusion.5 = f32[1310720]{0:T(1024)} fusion(s32[16384]{0:T(1024)S(1)} %bitcast.160, f32[16384]{0:T(1024)S(1)} %bitcast.161, f32[]{:T(128)} %constant.234.clone.1..sunk), kind=kCustom, calls=%fused_computation.5.clone.1 | custom fusion | flops 16384 | bytes 5242884 | tf_op jit(solution)/shard_map/while/body/eval_jaxpr/scatter-add | solution.py:80
  700.5 38.5 %while.135 = (s32[]{:T(128)}, f32[100,2560]{1,0:T(8,128)S(1)}, f32[2,100,2560]{2,0,1:T(2,128)}, f32[2,100]{1,0:T(2,128)S(1)}, f32[2,100,2560]{2,0,1:T(2,128)}, /*index=5*/s32[]{:T(128)}, s32[]{:T(128)}) while((s32[]{:T(128)}, f32[100,2560]{1,0:T(8,128)S(1)}, f32[2,100,2560]{2,0,1:T(2,128)}, f32[2,100]{1,0:T(2,128)S(1)}, ...), condition=%wide.region_18.19_spmd.clone, body=%wide.region_17.18_spmd.clone.sunk | while | flops 768003 | bytes 10241299 | solution.py:39
  704.3 15.4 %dynamic_update_slice.54 = f32[2,100,2560]{2,0,1:T(2,128)} dynamic-update-slice(f32[2,100,2560]{2,0,1:T(2,128)} %get-tuple-element.1522, f32[1,100,2560]{2,0,1:T(1,128)S(1)} %copy.108, s32[]{:T(128)} %get-tuple-element.1520, s32[]{:T(128)} %constant.233.clone.1..sunk.5, s32[]{:T(128)} %constant.233.clone.1..sunk.5) | dynamic-update-slice | bytes 2048004 | tf_op jit(solution)/shard_map/while/body/jit(dynamic_update_index_in_dim)/dynamic_update_slice | solution.py:39
  723.6 15.4 %dynamic_update_slice.54 = f32[2,100,2560]{2,0,1:T(2,128)} dynamic-update-slice(f32[2,100,2560]{2,0,1:T(2,128)} %get-tuple-element.1522, f32[1,100,2560]{2,0,1:T(1,128)S(1)} %copy.108, s32[]{:T(128)} %get-tuple-element.1520, s32[]{:T(128)} %constant.233.clone.1..sunk.5, s32[]{:T(128)} %constant.233.clone.1..sunk.5) | dynamic-update-slice | bytes 2048004 | tf_op jit(solution)/shard_map/while/body/jit(dynamic_update_index_in_dim)/dynamic_update_slice | solution.py:39
  755.6 16.6 %reshape.123 = f32[512,200]{1,0:T(8,128)} reshape(f32[512,100,2]{2,1,0:T(8,128)} %bitcast.155) | data formatting | bytes 819200
  772.5 82.1 %all-gather.19.cloned.1.call-done = f32[32,100,2560]{2,1,0:T(8,128)} async-done(((f32[1,100,2560]{2,1,0:T(8,128)}), f32[32,100,2560]{2,1,0:T(8,128)}) %all-gather.19.cloned.1.call-update) | async-done | bytes 32768016 | tf_op jit(solution)/shard_map/all_gather | solution.py:9
  854.6 50.2 %while.136 = (s32[]{:T(128)}, f32[100,2560]{1,0:T(8,128)S(1)}, s32[]{:T(128)}, f32[32,100]{1,0:T(8,128)S(1)}, f32[32,100,2560]{2,1,0:T(8,128)}, /*index=5*/s32[]{:T(128)}, s32[]{:T(128)}) while((s32[]{:T(128)}, f32[100,2560]{1,0:T(8,128)S(1)}, s32[]{:T(128)}, f32[32,100]{1,0:T(8,128)S(1)}, f32[32,100,2560]{2,1,0:T(8,128)}, ...), condition=%wide.region_21.22_spmd.clone, body=%wide.region_20.21_spmd.clone.sunk | while | flops 1024004 | bytes 3073305 | solution.py:21
  916.0 38.5 %while.137 = (s32[]{:T(128)}, f32[100,2560]{1,0:T(8,128)S(1)}, f32[2,100,2560]{2,0,1:T(2,128)}, f32[2,100]{1,0:T(2,128)S(1)}, f32[2,100,2560]{2,0,1:T(2,128)}, /*index=5*/s32[]{:T(128)}, s32[]{:T(128)}) while((s32[]{:T(128)}, f32[100,2560]{1,0:T(8,128)S(1)}, f32[2,100,2560]{2,0,1:T(2,128)}, f32[2,100]{1,0:T(2,128)S(1)}, ...), condition=%wide.region_23.24_spmd.clone, body=%wide.region_22.23_spmd.clone.sunk | while | flops 768004 | bytes 10241311 | solution.py:39
  919.8 15.4 %dynamic_update_slice.55 = f32[2,100,2560]{2,0,1:T(2,128)} dynamic-update-slice(f32[2,100,2560]{2,0,1:T(2,128)} %get-tuple-element.1564, f32[1,100,2560]{2,0,1:T(1,128)S(1)} %copy.109, s32[]{:T(128)S(6)} %sub.96, s32[]{:T(128)} %constant.233.clone.1..sunk.7, s32[]{:T(128)} %constant.233.clone.1..sunk.7) | dynamic-update-slice | bytes 2048004 | tf_op jit(solution)/shard_map/while/body/jit(dynamic_update_index_in_dim)/dynamic_update_slice | solution.py:39
  939.0 15.4 %dynamic_update_slice.55 = f32[2,100,2560]{2,0,1:T(2,128)} dynamic-update-slice(f32[2,100,2560]{2,0,1:T(2,128)} %get-tuple-element.1564, f32[1,100,2560]{2,0,1:T(1,128)S(1)} %copy.109, s32[]{:T(128)S(6)} %sub.96, s32[]{:T(128)} %constant.233.clone.1..sunk.7, s32[]{:T(128)} %constant.233.clone.1..sunk.7) | dynamic-update-slice | bytes 2048004 | tf_op jit(solution)/shard_map/while/body/jit(dynamic_update_index_in_dim)/dynamic_update_slice | solution.py:39
  967.2 103.0 %all-gather.21.cloned.1.call-done = f32[32,100,2560]{2,1,0:T(8,128)} async-done(((f32[1,100,2560]{2,1,0:T(8,128)}), f32[32,100,2560]{2,1,0:T(8,128)}) %all-gather.21.cloned.1.call-update) | async-done | bytes 32768016 | tf_op jit(solution)/shard_map/all_gather | solution.py:9
  1070.2 22.8 %reverse.2 = f32[32,100,2560]{2,1,0:T(8,128)} reverse(f32[32,100,2560]{2,1,0:T(8,128)} %all-gather.21.cloned.1.call-done), dimensions={0} | reverse | bytes 65536000 | tf_op jit(solution)/shard_map/rev | solution.py:11
  1093.0 50.2 %while.138 = (s32[]{:T(128)}, f32[100,2560]{1,0:T(8,128)S(1)}, s32[]{:T(128)}, f32[32,100]{1,0:T(8,128)S(1)}, f32[32,100,2560]{2,1,0:T(8,128)}, /*index=5*/s32[]{:T(128)}, s32[]{:T(128)}) while((s32[]{:T(128)}, f32[100,2560]{1,0:T(8,128)S(1)}, s32[]{:T(128)}, f32[32,100]{1,0:T(8,128)S(1)}, f32[32,100,2560]{2,1,0:T(8,128)}, ...), condition=%wide.region_26.27_spmd.clone, body=%wide.region_25.26_spmd.clone.sunk | while | flops 1024004 | bytes 3073305 | solution.py:21
  (429 shorter events, 367.5 us)
Async XLA Ops:
  7.2 175.6 %all-gather.15.cloned.1.call-start = ((), (), s32[]{:S(2)}) async-start(), calls=%async_computation.1 | async-start | bytes 35143680 | tf_op jit(solution)/shard_map/all_gather | solution.py:9
  8.1 3.7 copy-start.10
  13.7 39.5 %copy-start.25 = (u32[128]{0:T(128)S(1)}, u32[128]{0:T(128)}, u32[]{:S(2)}) copy-start(u32[128]{0:T(128)} %constant.253) | copy-start | bytes 1540
  53.1 311.1 %all-gather.17.cloned.1.call-start = ((), (), s32[]{:S(2)}) async-start(), calls=%async_computation.2 | async-start | bytes 35143680 | tf_op jit(solution)/shard_map/all_gather | solution.py:9
  182.6 50.3 %copy-start.12 = (f32[2,100]{0,1:T(8,128)}, f32[2,100]{0,1:T(8,128)S(1)}, u32[]{:S(2)}) copy-start(f32[2,100]{0,1:T(8,128)S(1)} %copy.46) | copy-start | bytes 2404
  232.9 3.9 copy-start.17
  246.9 607.7 %all-gather.19.cloned.1.call-start = ((), (), s32[]{:S(2)}) async-start(), calls=%async_computation.3 | async-start | bytes 35143680 | tf_op jit(solution)/shard_map/all_gather | solution.py:9
  438.9 3.5 copy-start.9
  438.9 3.5 copy-start.24
  539.8 3.5 copy-start.5
  544.0 2.3 copy-start.6
  660.2 3.5 copy-start.5
  664.3 2.3 copy-start.6
  683.1 10.7 copy-start.7
  683.1 10.7 copy-start.16
  698.7 1.8 copy-start.20
  700.5 39.7 %copy-start.22 = (f32[2,100]{1,0:T(2,128)S(1)}, f32[2,100]{1,0:T(2,128)}, u32[]{:S(2)}) copy-start(f32[2,100]{1,0:T(2,128)} %param.27) | copy-start | bytes 2404
  740.1 215.7 %reduce-scatter.4.cloned.1.call-start = ((), (), s32[]{:S(2)}) async-start(), calls=%async_computation.5 | async-start | bytes 655360
  772.2 298.0 %all-gather.21.cloned.1.call-start = ((), (), s32[]{:S(2)}) async-start(), calls=%async_computation.4 | async-start | bytes 35143680 | tf_op jit(solution)/shard_map/all_gather | solution.py:9
  854.6 50.2 %copy-start.13 = (f32[2,100]{0,1:T(8,128)S(1)}, f32[2,100]{0,1:T(8,128)}, u32[]{:S(2)}) copy-start(f32[2,100]{0,1:T(8,128)} %copy-done.12) | copy-start | bytes 2404
  916.0 39.5 %copy-start.18 = (f32[32,100]{1,0:T(8,128)S(1)}, f32[32,100]{1,0:T(8,128)}, u32[]{:S(2)}) copy-start(f32[32,100]{1,0:T(8,128)} %copy-done.17) | copy-start | bytes 38404
  916.0 39.6 %copy-start.23 = (pred[2]{0:T(512)(128)(4,1)S(1)}, pred[2]{0:T(512)(128)(4,1)}, u32[]{:S(2)}) copy-start(pred[2]{0:T(512)(128)(4,1)} %constant.238.clone.1) | copy-start | bytes 10
  1093.0 50.3 %copy-start.8 = (f32[2,100,2560]{2,0,1:T(2,128)S(1)}, f32[2,100,2560]{2,0,1:T(2,128)}, u32[]{:S(2)}) copy-start(f32[2,100,2560]{2,0,1:T(2,128)} %get-tuple-element.712) | copy-start | bytes 6144004
  1093.0 50.3 %copy-start.11 = (f32[2,100]{0,1:T(8,128)S(1)}, f32[2,100]{0,1:T(8,128)}, u32[]{:S(2)}) copy-start(f32[2,100]{0,1:T(8,128)} %copy-done.10) | copy-start | bytes 2404
  (11 other events, 12.7 us)
Sparse Core Ops, SparseCore 0:
  53.2 119.7 all-gather.14
  247.1 117.1 all-gather.16
  740.2 114.3 all-gather.18
  856.8 18.5 reduce-scatter.3
  955.6 114.5 all-gather.20
where the time goes:
time: 1170 us; the launch traced here: 1150 us
  other arithmetic  413 us (35%)
  waiting for transfers between devices  300 us (26%)
  local copies, waits for them, and re-layouts  274 us (23%)
  blocking collectives  136 us (12%)
  between operations  14.6 us (1%)
    all_gather x4, waiting for transfers between devices, carried_in(): pieces = jax.tree.map(lambda part: lax.all_gather(part, axis), value)  300 us
    select_n x124, other arithmetic, lap(): jnp.where(position < mine, new, old)  195 us
    scatter-add x2, other arithmetic, slice_terms(): flat_counts = jnp.zeros((doc_count * vocab_dev,), jnp.float32).at[flat_in...  177 us
    dynamic_update_slice x16, local copies, waits for them, and re-layouts, local_chain(): lax.scan(advance, incoming, (factors, added), reverse=reverse)  132 us
    unnamed x1, blocking collectives  128 us
    unnamed x56, local copies, waits for them, and re-layouts  47.7 us
    rev x4, local copies, waits for them, and re-layouts, carried_in(): pieces = jax.tree.map(lambda part: part[::-1], pieces)  45.6 us
  transfers between devices with their start and end apart: 5, of which 3 were waited for; matrix products, arithmetic and copies ran while one was open for 13% of the time, Pallas kernels for 0%

commit v1 on v0

v1 whole, which is shorter than its diff:
```python
import functools

import jax
import jax.numpy as jnp
from jax import lax
from jax.experimental import pallas as pl
from jax.experimental.pallas import tpu as pltpu
from jax.sharding import PartitionSpec as P

MESH = pl.DeviceIdType.MESH
ROWS = 8
LANES = 128
TILE_W = 256
TILE_D = 256
WORD_SPAN = 4096
M_IN, A1, M_OUT, B0, B1, N_IN, C0, N_OUT, E0, E1, X0, X1, DEV_D, DEV_G, DEV_Q = range(15)


def greet(peers):
    barrier = pltpu.get_barrier_semaphore()
    for count, peer in peers:
        def hello(k, _, peer=peer):
            pl.semaphore_signal(barrier, inc=1, device_id=peer(k), device_id_type=MESH)
            return 0
        lax.fori_loop(0, count, hello, 0)
    pl.semaphore_wait(barrier, sum(count for count, _ in peers))


def spread_coefs(coef_ref, table, spread):
    table[...] = jnp.zeros_like(table)
    table[0:16, :] = coef_ref[...]
    row = lambda i: coef_ref[i : i + 1, :]
    entry = row(A1) * row(M_IN)
    table[DEV_D : DEV_D + 1, :] = row(M_OUT) * entry
    table[DEV_G : DEV_G + 1, :] = row(N_OUT) * row(C0) * row(N_IN)
    table[DEV_Q : DEV_Q + 1, :] = row(N_OUT) * (row(C0) * (row(E1) * entry) + row(E0) * row(M_IN))
    spread[...] = table[...].T


def two_sided(chips, chip, core, half, tiles, spread, source, finish, bufs):
    (psend, precv, mine, cbuf, rbuf, obuf, wbuf, gsend, grecv,
     pair_sem, out_send, out_recv, back_send, back_recv, give_send, give_recv) = bufs
    first = core == 0
    partner = {"tm": 2 * chip + 1 - core}
    own = pl.ds(pl.multiple_of(core * half, LANES), half)
    other = pl.ds(pl.multiple_of((1 - core) * half, LANES), half)
    lane = lax.broadcasted_iota(jnp.int32, (ROWS, LANES), 1)

    def rows_of(r):
        return pl.ds(pl.multiple_of(r * ROWS, ROWS), ROWS)

    def col(r, i):
        return spread[rows_of(r), i : i + 1]

    def ends(r, lanes):
        rows = rows_of(r)
        p0 = col(r, B0) * source(0, r, rows, lanes)
        p1 = col(r, A1) * p0 + col(r, B1) * source(1, r, rows, lanes)
        q0 = col(r, C0) * (col(r, E1) * p1) + col(r, E0) * p0
        return col(r, M_OUT) * p1, col(r, N_OUT) * q0

    def give_ends(r, _):
        f, b = ends(r, other)
        psend[rows_of(r), 0:half] = f
        psend[rows_of(r), half : 2 * half] = b
        psend[rows_of(r), 2 * half :] = spread[rows_of(r), :]
        return 0

    lax.fori_loop(0, tiles, give_ends, 0)
    swap = pltpu.make_async_remote_copy(
        src_ref=psend, dst_ref=precv, send_sem=pair_sem.at[0], recv_sem=pair_sem.at[1],
        device_id=partner, device_id_type=MESH)
    swap.start()

    def keep_ends(r, _):
        f, b = ends(r, own)
        mine[rows_of(r), 0:half] = f
        mine[rows_of(r), half : 2 * half] = b
        return 0

    lax.fori_loop(0, tiles, keep_ends, 0)
    swap.wait_recv()

    def scalars(r):
        def both(i):
            a = col(r, i)
            b = precv[rows_of(r), 2 * half + i : 2 * half + i + 1]
            return jnp.where(first, a, b), jnp.where(first, b, a)
        return both(DEV_D), both(DEV_G), both(DEV_Q)

    def halves(r, lo, hi):
        a = mine[rows_of(r), lo:hi]
        b = precv[rows_of(r), lo:hi]
        return a, b

    def out_copy(r):
        return pltpu.make_async_remote_copy(
            src_ref=cbuf.at[rows_of(r)], dst_ref=rbuf.at[chip], send_sem=out_send.at[r], recv_sem=out_recv.at[chip],
            device_id={"tm": 2 * r + core}, device_id_type=MESH)

    def send_chip(k, _):
        r = lax.rem(chip + 1 + k, tiles)
        (d0, d1), (g0, g1), (q0, q1) = scalars(r)
        fa, fb = halves(r, 0, half)
        ba, bb = halves(r, half, 2 * half)
        f0, f1 = jnp.where(first, fa, fb), jnp.where(first, fb, fa)
        b0, b1 = jnp.where(first, ba, bb), jnp.where(first, bb, ba)
        whole = jnp.where(lane == 0, d0 * d1, jnp.where(lane == 1, g0 * g1, g0 * q1 * d0 + q0))
        f_chip = d1 * f0 + f1
        b_chip = g0 * (b1 + q1 * f0) + b0

        @pl.when(r != chip)
        def _():
            cbuf[rows_of(r), 0:half] = f_chip
            cbuf[rows_of(r), half : 2 * half] = b_chip
            cbuf[rows_of(r), 2 * half :] = whole
            out_copy(r).start()

        @pl.when(r == chip)
        def _():
            rbuf[chip, :, 0:half] = f_chip
            rbuf[chip, :, half : 2 * half] = b_chip
            rbuf[chip, :, 2 * half :] = whole

        return 0

    lax.fori_loop(0, tiles, send_chip, 0)

    def back_copy(c):
        return pltpu.make_async_remote_copy(
            src_ref=obuf.at[c], dst_ref=wbuf.at[rows_of(chip)], send_sem=back_send.at[c], recv_sem=back_recv.at[chip],
            device_id={"tm": 2 * c + core}, device_id_type=MESH)

    @pl.when(chip < tiles)
    def _():
        def arrive(k, _):
            src = lax.rem(chip + k, chips)
            pltpu.make_async_remote_copy(
                src_ref=rbuf.at[src], dst_ref=rbuf.at[src], send_sem=out_send.at[0], recv_sem=out_recv.at[src],
                device_id={"tm": 2 * src + core}, device_id_type=MESH).wait_recv()
            return 0

        lax.fori_loop(1, chips, arrive, 0)

        def onward(c, f):
            obuf[c, :, 0:half] = f
            return rbuf[c, :, 2 * half : 2 * half + 1] * f + rbuf[c, :, 0:half]

        lax.fori_loop(0, chips, onward, jnp.zeros((ROWS, half), jnp.float32))

        def homeward(k, s):
            c = chips - 1 - k
            f = obuf[c, :, 0:half]
            obuf[c, :, half : 2 * half] = s

            @pl.when(c != chip)
            def _():
                back_copy(c).start()

            @pl.when(c == chip)
            def _():
                wbuf[rows_of(chip), 0:half] = f
                wbuf[rows_of(chip), half : 2 * half] = s

            return (rbuf[c, :, 2 * half + 1 : 2 * half + 2] * s + rbuf[c, :, half : 2 * half]
                    + rbuf[c, :, 2 * half + 2 : 2 * half + 3] * f)

        lax.fori_loop(0, chips, homeward, jnp.zeros((ROWS, half), jnp.float32))

    def give_copy(r):
        return pltpu.make_async_remote_copy(
            src_ref=gsend.at[rows_of(r)], dst_ref=grecv.at[rows_of(r)], send_sem=give_send.at[r],
            recv_sem=give_recv.at[r], device_id=partner, device_id_type=MESH)

    def resolve(r, lanes, f, s):
        rows = rows_of(r)
        p0 = col(r, M_IN) * f + col(r, B0) * source(0, r, rows, lanes)
        p1 = col(r, A1) * p0 + col(r, B1) * source(1, r, rows, lanes)
        q1 = col(r, N_IN) * s + col(r, E1) * p1
        finish(1, r, rows, lanes, q1)
        finish(0, r, rows, lanes, col(r, C0) * q1 + col(r, E0) * p0)

    def own_half(k, _):
        r = lax.rem(chip + tiles - lax.rem(k, tiles), tiles)

        @pl.when(r != chip)
        def _():
            pltpu.make_async_remote_copy(
                src_ref=wbuf.at[rows_of(r)], dst_ref=wbuf.at[rows_of(r)], send_sem=back_send.at[0],
                recv_sem=back_recv.at[r], device_id={"tm": 2 * r + core}, device_id_type=MESH).wait_recv()

        (d0, _), (_, g1), (_, q1) = scalars(r)
        f = wbuf[rows_of(r), 0:half]
        s = wbuf[rows_of(r), half : 2 * half]
        fa, fb = halves(r, 0, half)
        ba, bb = halves(r, half, 2 * half)
        f_mid = d0 * f + jnp.where(first, fa, fb)
        s_mid = g1 * s + jnp.where(first, bb, ba) + q1 * f_mid
        gsend[rows_of(r), 0:half] = jnp.where(first, f_mid, f)
        gsend[rows_of(r), half : 2 * half] = jnp.where(first, s, s_mid)
        give_copy(r).start()
        resolve(r, own, jnp.where(first, f, f_mid), jnp.where(first, s_mid, s))
        return 0

    lax.fori_loop(0, tiles, own_half, 0)

    def other_half(k, _):
        r = lax.rem(chip + tiles - lax.rem(k, tiles), tiles)
        give_copy(r).wait_recv()
        resolve(r, other, grecv[rows_of(r), 0:half], grecv[rows_of(r), half : 2 * half])
        return 0

    lax.fori_loop(0, tiles, other_half, 0)

    swap.wait_send()

    def drain(r, _):
        give_copy(r).wait_send()

        @pl.when(r != chip)
        def _():
            out_copy(r).wait_send()

        return 0

    lax.fori_loop(0, tiles, drain, 0)

    @pl.when(chip < tiles)
    def _():
        def drain_back(k, _):
            back_copy(lax.rem(chip + k, chips)).wait_send()
            return 0

        lax.fori_loop(1, chips, drain_back, 0)


def chain_peers(chips, chip, core):
    return [
        (chips - 1, lambda k: {"tm": 2 * lax.rem(chip + 1 + k, chips) + core}),
        (1, lambda k: {"tm": 2 * chip + 1 - core}),
    ]


def chain_scratch(chips, half, tiles):
    wide, full = 2 * half + LANES, tiles * ROWS
    f32 = jnp.float32
    dma = pltpu.SemaphoreType.DMA
    return [
        pltpu.VMEM((LANES, LANES), f32), pltpu.VMEM((LANES, LANES), f32),
        pltpu.VMEM((full, wide), f32), pltpu.VMEM((full, wide), f32), pltpu.VMEM((full, 2 * half), f32),
        pltpu.VMEM((full, wide), f32), pltpu.VMEM((chips, ROWS, wide), f32),
        pltpu.VMEM((chips, ROWS, 2 * half), f32), pltpu.VMEM((full, 2 * half), f32),
        pltpu.VMEM((full, 2 * half), f32), pltpu.VMEM((full, 2 * half), f32),
        dma((2,)), dma((tiles,)), dma((chips,)), dma((chips,)), dma((tiles,)), dma((tiles,)), dma((tiles,)),
    ]


def smooth_kernel(chips, topics, x_hbm, coef_ref, tw_ref, raw, xs, load_sem, table, spread, *bufs):
    core, chip = lax.rem(lax.axis_index("tm"), 2), lax.axis_index("tm") // 2
    half, tiles = xs.shape[2] // 2, xs.shape[1] // ROWS
    load = pltpu.make_async_copy(x_hbm, raw, load_sem.at[0])
    load.start()
    spread_coefs(coef_ref, table, spread)
    greet(chain_peers(chips, chip, core))
    load.wait()
    even = topics // ROWS * ROWS

    def move(r, _):
        rows = pl.ds(pl.multiple_of(r * ROWS, ROWS), ROWS)
        for s in range(2):
            xs[s, rows, :] = raw[s, rows, :]
        return 0

    lax.fori_loop(0, topics // ROWS, move, 0)
    if even < topics:
        xs[:, even:, :] = jnp.zeros((2, ROWS, 2 * half), jnp.float32)
        xs[:, even:topics, :] = raw[:, even:, :]

    def source(s, r, rows, lanes):
        return xs[s, rows, lanes]

    def finish(s, r, rows, lanes, q):
        tw_ref[s, rows, lanes] = jnp.exp(q - spread[rows, X0 + s : X0 + s + 1])

    two_sided(chips, chip, core, half, tiles, spread, source, finish, bufs)


def adjoint_kernel(chips, shares, e_hbm, t_hbm, tot_ref, sums_ref, coef_ref, out_ref, own_ref,
                   es, ts, load_sem, totals, tot_in, sums_in, tot_sem, sum_sem, table, spread, *bufs):
    core, chip = lax.rem(lax.axis_index("tm"), 2), lax.axis_index("tm") // 2
    share = lax.axis_index("word")
    half, tiles = es.shape[2] // 2, es.shape[1] // ROWS
    loads = [pltpu.make_async_copy(e_hbm, es, load_sem.at[0]), pltpu.make_async_copy(t_hbm, ts, load_sem.at[1])]
    for load in loads:
        load.start()
    spread_coefs(coef_ref, table, spread)
    neighbour = lambda k: {"word": lax.rem(share + 1 + k, shares)}
    greet(chain_peers(chips, chip, core) + [(shares - 1, neighbour)])

    def tot_copy(k):
        return pltpu.make_async_remote_copy(
            src_ref=tot_ref, dst_ref=tot_in.at[shares - 2 - k], send_sem=tot_sem.at[0, k],
            recv_sem=tot_sem.at[1, shares - 2 - k], device_id=neighbour(k), device_id_type=MESH)

    def sum_copy(k):
        return pltpu.make_async_remote_copy(
            src_ref=sums_ref.at[lax.rem(share + 1 + k, shares)], dst_ref=sums_in.at[shares - 2 - k],
            send_sem=sum_sem.at[0, k], recv_sem=sum_sem.at[1, shares - 2 - k],
            device_id=neighbour(k), device_id_type=MESH)

    for k in range(shares - 1):
        tot_copy(k).start()
    for k in range(shares - 1):
        sum_copy(k).start()
    for load in loads:
        load.wait()
    total = tot_ref[...]
    for k in range(shares - 1):
        tot_copy(shares - 2 - k).wait_recv()
        total = total + tot_in[k]
    totals[...] = total

    def source(s, r, rows, lanes):
        return es[s, rows, lanes] - totals[rows, s : s + 1] * ts[s, rows, lanes]

    def finish(s, r, rows, lanes, q):
        out_ref[s, rows, lanes] = spread[rows, X0 + s : X0 + s + 1] * q

    two_sided(chips, chip, core, half, tiles, spread, source, finish, bufs)
    sums = sums_ref[share]
    for k in range(shares - 1):
        sum_copy(shares - 2 - k).wait_recv()
        sums = sums + sums_in[k]
    own_ref[...] = sums
    for k in range(shares - 1):
        tot_copy(k).wait_send()
        sum_copy(k).wait_send()


def sort_entries(x):
    groups = x.shape[0]
    shape = (groups * 16, 8, 128)
    x = x.reshape(shape)
    sub = lax.broadcasted_iota(jnp.int32, (8, 128), 0)
    lane = lax.broadcasted_iota(jnp.int32, (8, 128), 1)

    def bit_of(j):
        return (sub >> (j - 4)) & 1 if j < 7 else (lane >> (j - 7)) & 1

    def flip(x, k):
        if k >= 14:
            return x
        if k >= 4:
            return x ^ (-bit_of(k))[None]
        pieces = x.reshape((groups * 16 >> (k + 1), 2, 1 << k, 8, 128))
        return jnp.stack([pieces[:, 0], ~pieces[:, 1]], axis=1).reshape(shape)

    def exchange(x, j):
        if j < 4:
            pieces = x.reshape((groups * 16 >> (j + 1), 2, 1 << j, 8, 128))
            a, b = pieces[:, 0], pieces[:, 1]
            return jnp.stack([jnp.minimum(a, b), jnp.maximum(a, b)], axis=1).reshape(shape)
        low = (bit_of(j) == 0)[None]
        if j < 7:
            step, size, axis = 1 << (j - 4), 8, 1
            y = x
        else:
            step, size, axis = 1 << (j - 7), 128, 1
            y = x.reshape((groups * 16 * 8, 128))
        ahead = pltpu.roll(y, size - step, axis).reshape(shape)
        partner = ahead
        if 2 * step != size:
            partner = jnp.where(low, ahead, pltpu.roll(y, step, axis).reshape(shape))
        return jnp.where(low, jnp.minimum(x, partner), jnp.maximum(x, partner))

    for k in range(1, 15):
        x = flip(x, k)
        for j in range(k - 1, -1, -1):
            x = exchange(x, j)
        x = flip(x, k)
    return x.reshape((groups, 16, 8, 128))


def tally_kernel(topics, tw_ref, w_ref, keys_ref, exp_ref, tot_ref, sums_ref,
                 ordered, bounds, w32, wt, wb, tr, acc, ratio, sums, tots):
    slices, full, words = tw_ref.shape
    docs = w_ref.shape[2]
    shares = sums_ref.shape[0]
    keys = sort_entries(keys_ref[...].reshape((slices, 16, 8, 128)))
    ordered[:, 128:, :] = jnp.full((slices, ordered.shape[1] - 128, 128), -1, jnp.int32)
    tiles = words // TILE_W
    blocks = docs // TILE_D
    for s in range(slices):
        ordered[s, 0:128, :] = keys[s].reshape((128, 128)).T
        least, most = keys[s, 0, 0:1, :], keys[s, 15, 7:8, :]
        for h in range(blocks):
            for j in range(tiles):
                low = (h * WORD_SPAN + j * TILE_W) << 12
                bounds[s, h, j, 0] = jnp.sum((most < low).astype(jnp.int32))
                bounds[s, h, j, 1] = jnp.sum((least < low + (TILE_W << 12)).astype(jnp.int32))

    w32[...] = jnp.zeros_like(w32)
    tr[topics // 16 * 16 :, :] = jnp.zeros((128 - topics // 16 * 16, words), jnp.bfloat16)
    lane = lax.broadcasted_iota(jnp.int32, tot_ref.shape, 1)
    place = lax.broadcasted_iota(jnp.int32, (TILE_W, 1), 0).astype(jnp.float32)

    def one_slice(s, _):
        w32[0:topics, :] = w_ref[s].astype(jnp.float32)
        wb[...] = w32[...].astype(jnp.bfloat16)
        wt[...] = w32[...].T.astype(jnp.bfloat16)
        tr[0:full, :] = tw_ref[s].astype(jnp.bfloat16)
        sums[...] = jnp.zeros_like(sums)
        tots[...] = jnp.zeros_like(tots)

        def one_tile(j, _):
            lanes = pl.ds(pl.multiple_of(j * TILE_W, TILE_W), TILE_W)
            topic = tr[:, lanes]
            for h in range(blocks):
                base = h * WORD_SPAN + j * TILE_W
                start, stop = bounds[s, h, j, 0], bounds[s, h, j, 1]
                acc[...] = jnp.zeros_like(acc)

                def pair(i, _):
                    at = start + 2 * i
                    key = jnp.concatenate(
                        [ordered[s, pl.ds(at, 1), :], ordered[s, pl.ds(at + 1, 1), :]], axis=1)
                    word = ((key >> 12) - base).astype(jnp.float32)
                    doc = ((key >> 4) & 255).astype(jnp.float32)
                    count = (key & 15).astype(jnp.float32)
                    docs_hot = jnp.where(place == doc, count, 0.0).astype(jnp.bfloat16)
                    words_hot = jnp.where(place == word, 1.0, 0.0).astype(jnp.bfloat16)
                    acc[...] += lax.dot_general(
                        docs_hot, words_hot, (((1,), (1,)), ((), ())), preferred_element_type=jnp.float32)
                    return 0

                lax.fori_loop(0, (stop - start + 1) // 2, pair, 0)
                mixture = jnp.dot(
                    wt[h * TILE_D : (h + 1) * TILE_D, :], topic, preferred_element_type=jnp.float32)
                ratio[h * TILE_D : (h + 1) * TILE_D, :] = (acc[...] / mixture).astype(jnp.bfloat16)
            sums[...] += lax.dot_general(
                topic, ratio[...], (((1,), (1,)), ((), ())), preferred_element_type=jnp.float32)
            weighted = jnp.dot(wb[...], ratio[...], preferred_element_type=jnp.float32)
            expected = topic[0:full].astype(jnp.float32) * weighted[0:full]
            exp_ref[s, :, lanes] = expected
            tots[...] += expected
            return 0

        lax.fori_loop(0, tiles, one_tile, 0)
        for y in range(shares):
            sums_ref[y, s] = sums[0:full, y * (docs // shares) : (y + 1) * (docs // shares)]
        total = jnp.sum(tots[...], axis=1, keepdims=True)
        tot_ref[...] = jnp.where(lane == s, total, jnp.where(s == 0, 0.0, tot_ref[...]))
        return 0

    lax.fori_loop(0, slices, one_slice, 0)


VMEM_SPEC = pl.BlockSpec(memory_space=pltpu.VMEM)
ANY_SPEC = pl.BlockSpec(memory_space=pl.ANY)
LIMIT = 60 * 1024 * 1024


def tally(topic_word, doc_weights, keys, topics, shares):
    slices, full, words = topic_word.shape
    docs = doc_weights.shape[2]
    f32, bf16 = jnp.float32, jnp.bfloat16
    return pl.pallas_call(
        functools.partial(tally_kernel, topics),
        out_shape=(
            jax.ShapeDtypeStruct((slices, full, words), f32),
            jax.ShapeDtypeStruct((full, LANES), f32),
            jax.ShapeDtypeStruct((shares, slices, full, docs // shares), f32),
        ),
        in_specs=[VMEM_SPEC] * 3,
        out_specs=(VMEM_SPEC,) * 3,
        scratch_shapes=[
            pltpu.VMEM((slices, 136, 128), jnp.int32),
            pltpu.SMEM((slices, docs // TILE_D, words // TILE_W, 2), jnp.int32),
            pltpu.VMEM((128, docs), f32), pltpu.VMEM((docs, 128), bf16), pltpu.VMEM((128, docs), bf16),
            pltpu.VMEM((128, words), bf16), pltpu.VMEM((TILE_D, TILE_W), f32), pltpu.VMEM((docs, TILE_W), bf16),
            pltpu.VMEM((128, docs), f32), pltpu.VMEM((full, TILE_W), f32),
        ],
        compiler_params=pltpu.CompilerParams(vmem_limit_bytes=LIMIT),
        name="tally",
    )(topic_word, doc_weights, keys)


def coef_rows(rows, topics):
    table = jnp.concatenate([r[None] for r in rows], axis=0)
    return jnp.pad(table, ((0, 16 - len(rows)), (0, LANES - topics)))


def make_local(chips, shares):
    def local(pseudo_obs, filter_decay, smooth_gain, log_norm, doc_weights, doc_ids, word_ids, counts):
        slices, topics, words = pseudo_obs.shape
        tiles, half = -(-topics // ROWS), words // 2
        full = tiles * ROWS
        docs = doc_weights.shape[2]
        entries = doc_ids.shape[1]
        f32 = jnp.float32
        positions = lax.axis_index("tm") * slices + jnp.arange(slices, dtype=jnp.int32)
        keep = jnp.where((positions == slices * 2 * chips - 1)[:, None], 1.0, 1.0 - smooth_gain)
        one = jnp.ones((topics,), f32)
        d0, d1 = filter_decay[0], filter_decay[1]
        g0, g1 = smooth_gain[0], smooth_gain[1]
        coef_a = coef_rows(
            [d0, d1, one, 1.0 - d0, 1.0 - d1, g1, g0, one, keep[0], keep[1], log_norm[0], log_norm[1]], topics)
        coef_b = coef_rows(
            [one, g0, g1, one, one, one, d1, d0, keep[0], keep[1], 1.0 - d0, 1.0 - d1], topics)
        word = word_ids - lax.axis_index("word") * words
        keys = ((doc_ids // TILE_D * WORD_SPAN + word) << 12) | ((doc_ids % TILE_D) << 4) | counts
        keys = keys.reshape((slices, 128, entries // 128))

        topic_word = pl.pallas_call(
            functools.partial(smooth_kernel, chips, topics),
            out_shape=jax.ShapeDtypeStruct((slices, full, words), f32),
            in_specs=[ANY_SPEC, VMEM_SPEC],
            out_specs=VMEM_SPEC,
            scratch_shapes=[
                pltpu.VMEM((slices, topics, words), f32), pltpu.VMEM((slices, full, words), f32),
                pltpu.SemaphoreType.DMA((1,)),
            ]
            + chain_scratch(chips, half, tiles),
            compiler_params=pltpu.CompilerParams(
                collective_id=0, has_side_effects=True, vmem_limit_bytes=LIMIT),
            name="smooth",
        )(pseudo_obs, coef_a)
        expected, totals, sums = tally(topic_word, doc_weights, keys, topics, shares)
        dma = pltpu.SemaphoreType.DMA
        grad, own_sums = pl.pallas_call(
            functools.partial(adjoint_kernel, chips, shares),
            out_shape=(
                jax.ShapeDtypeStruct((slices, full, words), f32),
                jax.ShapeDtypeStruct((slices, full, docs // shares), f32),
            ),
            in_specs=[ANY_SPEC, ANY_SPEC, VMEM_SPEC, VMEM_SPEC, VMEM_SPEC],
            out_specs=(VMEM_SPEC, VMEM_SPEC),
            scratch_shapes=[
                pltpu.VMEM((slices, full, words), f32), pltpu.VMEM((slices, full, words), f32), dma((2,)),
                pltpu.VMEM((full, LANES), f32), pltpu.VMEM((shares - 1, full, LANES), f32),
                pltpu.VMEM((shares - 1, slices, full, docs // shares), f32),
                dma((2, shares - 1)), dma((2, shares - 1)),
            ] + chain_scratch(chips, half, tiles),
            compiler_params=pltpu.CompilerParams(
                collective_id=1, has_side_effects=True, vmem_limit_bytes=LIMIT),
            name="adjoint",
        )(expected, topic_word, totals, sums, coef_b)
        own_docs = docs // shares
        own_weights = lax.dynamic_slice_in_dim(doc_weights, lax.axis_index("word") * own_docs, own_docs, 2)
        return grad[:, :topics], own_weights.astype(f32) * own_sums[:, :topics]

    return local


def solution(mesh):
    return jax.shard_map(
        make_local(mesh.shape["tm"] // 2, mesh.shape["word"]),
        mesh=mesh,
        in_specs=(
            P("tm", None, "word"),
            P("tm", None),
            P("tm", None),
            P("tm", None),
            P("tm", None, None),
            P("tm", "word"),
            P("tm", "word"),
            P("tm", "word"),
        ),
        out_specs=(P("tm", None, "word"), P("tm", None, "word")),
        check_vma=False,
    )
```

time: 1170 us -> 196 us (0.17); the launches traced: 1150 us -> 195 us
  other arithmetic: 413 us -> 4.03 us
  waiting for transfers between devices: 300 us -> 0 us
  local copies, waits for them, and re-layouts: 274 us -> 14.1 us
  Pallas kernels: 0 us -> 177 us
  blocking collectives: 136 us -> 0 us
  between operations: 14.6 us -> 0.68 us
    all_gather x4 -> x0, waiting for transfers between devices: 300 us -> none  [carried_in(): pieces = jax.tree.map(lambda part: lax.all_gather(part, axis), value)]
    select_n x127 -> x1, other arithmetic: 198 us -> 0.75 us  [local(): jnp.where((positions == slices * 2 * chips - 1)[:, None], 1.0, 1.0 - smoo...]
    scatter-add x2 -> x0, other arithmetic: 177 us -> none  [slice_terms(): flat_counts = jnp.zeros((doc_count * vocab_dev,), jnp.float32).at[flat_in...]
    pallas_call x0 -> x3, Pallas kernels: none -> 177 us  [the longest x1 62.7 us: local(): pl.pallas_call(functools.partial(adjoint_kernel, chips, shares), out_shap...]
    dynamic_update_slice x16 -> x0, local copies, waits for them, and re-layouts: 132 us -> none  [local_chain(): lax.scan(advance, incoming, (factors, added), reverse=reverse)]
    unnamed x1 -> x0, blocking collectives: 128 us -> none
    rev x7 -> x0, local copies, waits for them, and re-layouts: 45.7 us -> none  [the longest x4 45.6 us: carried_in(): pieces = jax.tree.map(lambda part: part[::-1], pieces)]
    unnamed x56 -> x5, local copies, waits for them, and re-layouts: 47.7 us -> 10.8 us
  transfers between devices with their start and end apart: 5 -> 0, of which waited for: 3 -> 0; matrix products, arithmetic and copies ran while one was open for 13% -> 0% of each run, Pallas kernels for 0% -> 0%
where the time goes in v1:
time: 196 us; the launch traced here: 195 us
  Pallas kernels  177 us (90%)
  local copies, waits for them, and re-layouts  14.1 us (7%)
  other arithmetic  4.03 us (2%)
    pallas_call x1, Pallas kernels, local(): pl.pallas_call(functools.partial(adjoint_kernel, chips, shares), out_shap...  62.7 us
    pallas_call x1, Pallas kernels, tally(): pl.pallas_call(functools.partial(tally_kernel, topics), out_shape=(jax.Sh...  57 us
    pallas_call x1, Pallas kernels, local(): pl.pallas_call(functools.partial(smooth_kernel, chips, topics), out_shape...  56.8 us
    unnamed x5, local copies, waits for them, and re-layouts  10.8 us

profile of v1, /device:TPU:1, one launch (start us, length us, event | category | flops | bytes accessed | tf_op | source)
XLA Modules:
  0.0 195.3 jit_solution(10227004555046133313)
XLA Ops:
  0.6 0.8 subtract_select_fusion
  1.4 0.8 fusion.4
  2.2 0.7 concatenate.9
  2.9 0.6 pad.8.coef_ref
  3.5 1.4 concatenate.8
  4.9 0.6 pad.7.coef_ref
  5.5 1.6 fusion.3
  7.1 0.7 copy.17
  7.7 1.6 copy.11.w_ref
  9.4 3.3 %copy.10.x_hbm = f32[2,100,2560]{2,1,0:T(8,128)} copy(f32[2,100,2560]{2,0,1:T(2,128)} %param.8) | data formatting | bytes 4096000 | tf_op args[0]
  12.7 56.8 %smooth.1.tw_ref.t_hbm = f32[2,104,2560]{2,1,0:T(8,128)} custom-call(f32[2,100,2560]{2,1,0:T(8,128)} %copy.10.x_hbm, f32[16,128]{1,0:T(8,128)} %pad.7.coef_ref), custom_call_target="tpu_custom_call" | custom-call | tf_op jit(solution)/shard_map/smooth/pallas_call | solution.py:514
  69.5 57.0 %tally.1 = (f32[2,104,2560]{2,1,0:T(8,128)}, f32[104,128]{1,0:T(8,128)}, f32[4,2,104,128]{3,2,1,0:T(8,128)}) custom-call(f32[2,104,2560]{2,1,0:T(8,128)} %smooth.1.tw_ref.t_hbm, bf16[2,100,512]{2,1,0:T(8,128)(2,1)} %copy.11.w_ref, s32[2,128,128]{2,1,0:T(8,128)} %bitcast.7), custom_call_target="tpu_custom_call" | custom-call | tf_op jit(solution)/shard_map/tally/pallas_call | solution.py:467
  126.5 62.7 %adjoint.1 = (f32[2,104,2560]{2,1,0:T(8,128)}, f32[2,104,128]{2,1,0:T(8,128)}) custom-call(f32[2,104,2560]{2,1,0:T(8,128)} %get-tuple-element.7.e_hbm, f32[2,104,2560]{2,1,0:T(8,128)} %smooth.1.tw_ref.t_hbm, f32[104,128]{1,0:T(8,128)} %get-tuple-element.8.tot_ref, f32[4,2,104,128]{3,2,1,0:T(8,128)} %get-tuple-element.9.sums_ref, f32[16,128]{1,0:T(8,128)} %pad.8.coef_ref), custom_call_target="tpu_custom_call" | custom-call | tf_op jit(solution)/shard_map/adjoint/pallas_call | solution.py:530
  189.2 0.9 slice_multiply_fusion
  190.1 0.7 copy.14
  190.8 4.5 %copy.13 = f32[2,100,2560]{2,0,1:T(2,128)} copy(f32[2,100,2560]{2,1,0:T(8,128)} %bitcast.6) | data formatting | bytes 4096000
  (3 shorter events, 0.0 us)

commit v2 on v1

v2 whole, which is shorter than its diff:
```python
import functools

import jax
import jax.numpy as jnp
from jax import lax
from jax.experimental import pallas as pl
from jax.experimental.pallas import tpu as pltpu
from jax.sharding import PartitionSpec as P

MESH = pl.DeviceIdType.MESH
ROWS = 8
LANES = 128
TILE_W = 256
TILE_D = 256
WORD_SPAN = 4096
SPARE = 136
DEEP = 4
CHUNKS = 2
M_IN, A1, M_OUT, B0, B1, N_IN, C0, N_OUT, E0, E1, X0, X1, DEV_D, DEV_G, DEV_Q = range(15)


def greet(peers):
    barrier = pltpu.get_barrier_semaphore()
    for count, peer in peers:
        def hello(k, _, peer=peer):
            pl.semaphore_signal(barrier, inc=1, device_id=peer(k), device_id_type=MESH)
            return 0
        lax.fori_loop(0, count, hello, 0)
    pl.semaphore_wait(barrier, sum(count for count, _ in peers))


def spread_coefs(rows, table, spread):
    entry = rows[A1] * rows[M_IN]
    rows = rows + [
        rows[M_OUT] * entry,
        rows[N_OUT] * rows[C0] * rows[N_IN],
        rows[N_OUT] * (rows[C0] * (rows[E1] * entry) + rows[E0] * rows[M_IN]),
    ]
    table[...] = jnp.zeros_like(table)
    for i, row in enumerate(rows):
        table[i : i + 1, 0 : row.shape[1]] = row
    spread[...] = table[...].T


def keep_rows(gain_ref, slices_all):
    slices = gain_ref.shape[0]
    at = lax.axis_index("tm") * slices
    return [
        jnp.where(at + s == slices_all - 1, 1.0, 1.0 - gain_ref[s : s + 1, :]) for s in range(slices)
    ]


def owner_maps(chips, tiles):
    if chips == 16 and tiles == 13:
        return lambda r: r + (r + 3) // 4, lambda c: c - (c + 3) // 5, lambda c: lax.rem(c, 5) != 1
    return lambda r: r, lambda c: c, lambda c: c < tiles


def two_sided(chips, chip, core, half, tiles, spread, source, finish, meanwhile, bufs):
    (psend, precv, mine, cbuf, rbuf, obuf, wbuf, gsend, grecv,
     pair_send, pair_recv, out_send, out_recv, back_send, back_recv, give_send, give_recv) = bufs
    first = core == 0
    width = half // CHUNKS
    partner = {"tm": 2 * chip + 1 - core}
    chip_of, tile_of, owns = owner_maps(chips, tiles)
    is_owner = owns(chip)
    my_tile = tile_of(chip)
    lane = lax.broadcasted_iota(jnp.int32, (ROWS, LANES), 1)

    def rows_of(r):
        return pl.ds(pl.multiple_of(r * ROWS, ROWS), ROWS)

    def col(r, i):
        return spread[rows_of(r), i : i + 1]

    def span(ch):
        return 2 * width + (LANES if ch == 0 else 0)

    def ends(r, side, ch):
        p0 = col(r, B0) * source(0, r, side, ch)
        p1 = col(r, A1) * p0 + col(r, B1) * source(1, r, side, ch)
        q0 = col(r, C0) * (col(r, E1) * p1) + col(r, E0) * p0
        return col(r, M_OUT) * p1, col(r, N_OUT) * q0

    def swap(ch):
        return pltpu.make_async_remote_copy(
            src_ref=psend.at[ch, :, 0 : span(ch)], dst_ref=precv.at[ch, :, 0 : span(ch)],
            send_sem=pair_send.at[ch], recv_sem=pair_recv.at[ch], device_id=partner, device_id_type=MESH)

    for ch in range(CHUNKS):
        def give_ends(r, _, ch=ch):
            f, b = ends(r, 1 - core, ch)
            psend[ch, rows_of(r), 0:width] = f
            psend[ch, rows_of(r), width : 2 * width] = b
            if ch == 0:
                psend[ch, rows_of(r), 2 * width :] = spread[rows_of(r), :]
            return 0

        lax.fori_loop(0, tiles, give_ends, 0)
        swap(ch).start()

    for ch in range(CHUNKS):
        def keep_ends(r, _, ch=ch):
            f, b = ends(r, core, ch)
            mine[ch, rows_of(r), 0:width] = f
            mine[ch, rows_of(r), width : 2 * width] = b
            return 0

        lax.fori_loop(0, tiles, keep_ends, 0)

    def scalars(r):
        def both(i):
            a = col(r, i)
            b = precv[0, rows_of(r), 2 * width + i : 2 * width + i + 1]
            return jnp.where(first, a, b), jnp.where(first, b, a)
        return both(DEV_D), both(DEV_G), both(DEV_Q)

    def ordered_pair(r, ch, lo, hi):
        a = mine[ch, rows_of(r), lo:hi]
        b = precv[ch, rows_of(r), lo:hi]
        return jnp.where(first, a, b), jnp.where(first, b, a)

    def out_copy(r, ch):
        return pltpu.make_async_remote_copy(
            src_ref=cbuf.at[ch, rows_of(r), 0 : span(ch)], dst_ref=rbuf.at[ch, chip, :, 0 : span(ch)],
            send_sem=out_send.at[ch, r], recv_sem=out_recv.at[ch, chip],
            device_id={"tm": 2 * chip_of(r) + core}, device_id_type=MESH)

    for ch in range(CHUNKS):
        swap(ch).wait_recv()

        def send_chip(k, _, ch=ch):
            r = lax.rem(chip + 1 + k, tiles)
            (d0, d1), (g0, g1), (q0, q1) = scalars(r)
            f0, f1 = ordered_pair(r, ch, 0, width)
            b0, b1 = ordered_pair(r, ch, width, 2 * width)
            f_chip = d1 * f0 + f1
            b_chip = g0 * (b1 + q1 * f0) + b0
            cbuf[ch, rows_of(r), 0:width] = f_chip
            cbuf[ch, rows_of(r), width : 2 * width] = b_chip
            if ch == 0:
                cbuf[ch, rows_of(r), 2 * width :] = jnp.where(
                    lane == 0, d0 * d1, jnp.where(lane == 1, g0 * g1, g0 * q1 * d0 + q0))

            @pl.when(chip_of(r) != chip)
            def _():
                out_copy(r, ch).start()

            return 0

        lax.fori_loop(0, tiles, send_chip, 0)

    meanwhile()

    def back_copy(c, ch):
        return pltpu.make_async_remote_copy(
            src_ref=obuf.at[ch, c], dst_ref=wbuf.at[ch, rows_of(my_tile)],
            send_sem=back_send.at[ch, c], recv_sem=back_recv.at[ch, my_tile],
            device_id={"tm": 2 * c + core}, device_id_type=MESH)

    @pl.when(is_owner)
    def _():
        for ch in range(CHUNKS):
            rbuf[ch, chip, :, 0 : span(ch)] = cbuf[ch, rows_of(my_tile), 0 : span(ch)]

            def arrive(k, _, ch=ch):
                src = lax.rem(chip + k, chips)
                pltpu.make_async_remote_copy(
                    src_ref=cbuf.at[ch, 0:ROWS, 0 : span(ch)], dst_ref=rbuf.at[ch, src, :, 0 : span(ch)],
                    send_sem=out_send.at[ch, 0], recv_sem=out_recv.at[ch, src],
                    device_id={"tm": 2 * src + core}, device_id_type=MESH).wait_recv()
                return 0

            lax.fori_loop(1, chips, arrive, 0)

            def scalar(c, i):
                return rbuf[0, c, :, 2 * width + i : 2 * width + i + 1]

            def onward(c, f, ch=ch):
                obuf[ch, c, :, 0:width] = f
                return scalar(c, 0) * f + rbuf[ch, c, :, 0:width]

            lax.fori_loop(0, chips, onward, jnp.zeros((ROWS, width), jnp.float32))

            def homeward(k, s, ch=ch):
                c = chips - 1 - k
                f = obuf[ch, c, :, 0:width]
                obuf[ch, c, :, width : 2 * width] = s

                @pl.when(c != chip)
                def _():
                    back_copy(c, ch).start()

                return scalar(c, 1) * s + rbuf[ch, c, :, width : 2 * width] + scalar(c, 2) * f

            lax.fori_loop(0, chips, homeward, jnp.zeros((ROWS, width), jnp.float32))
            wbuf[ch, rows_of(my_tile), :] = obuf[ch, chip]

    def give_copy(r, ch):
        return pltpu.make_async_remote_copy(
            src_ref=gsend.at[ch, rows_of(r)], dst_ref=grecv.at[ch, rows_of(r)], send_sem=give_send.at[ch, r],
            recv_sem=give_recv.at[ch, r], device_id=partner, device_id_type=MESH)

    def resolve(r, side, ch, f, s):
        p0 = col(r, M_IN) * f + col(r, B0) * source(0, r, side, ch)
        p1 = col(r, A1) * p0 + col(r, B1) * source(1, r, side, ch)
        q1 = col(r, N_IN) * s + col(r, E1) * p1
        finish(1, r, side, ch, q1)
        finish(0, r, side, ch, col(r, C0) * q1 + col(r, E0) * p0)

    def turn(k):
        return lax.rem(my_tile + tiles - k, tiles)

    for ch in range(CHUNKS):
        def own_half(k, _, ch=ch):
            r = turn(k)

            @pl.when(chip_of(r) != chip)
            def _():
                pltpu.make_async_remote_copy(
                    src_ref=obuf.at[ch, 0], dst_ref=wbuf.at[ch, rows_of(r)], send_sem=back_send.at[ch, 0],
                    recv_sem=back_recv.at[ch, r], device_id=partner, device_id_type=MESH).wait_recv()

            (d0, _), (_, g1), (_, q1) = scalars(r)
            f = wbuf[ch, rows_of(r), 0:width]
            s = wbuf[ch, rows_of(r), width : 2 * width]
            f_mid = d0 * f + ordered_pair(r, ch, 0, width)[0]
            s_mid = g1 * s + ordered_pair(r, ch, width, 2 * width)[1] + q1 * f_mid
            gsend[ch, rows_of(r), 0:width] = jnp.where(first, f_mid, f)
            gsend[ch, rows_of(r), width : 2 * width] = jnp.where(first, s, s_mid)
            give_copy(r, ch).start()
            resolve(r, core, ch, jnp.where(first, f, f_mid), jnp.where(first, s_mid, s))
            return 0

        lax.fori_loop(0, tiles, own_half, 0)

    for ch in range(CHUNKS):
        def other_half(k, _, ch=ch):
            r = turn(k)
            give_copy(r, ch).wait_recv()
            resolve(r, 1 - core, ch, grecv[ch, rows_of(r), 0:width], grecv[ch, rows_of(r), width : 2 * width])
            return 0

        lax.fori_loop(0, tiles, other_half, 0)

    for ch in range(CHUNKS):
        swap(ch).wait_send()

        def drain(r, _, ch=ch):
            give_copy(r, ch).wait_send()

            @pl.when(chip_of(r) != chip)
            def _():
                out_copy(r, ch).wait_send()

            return 0

        lax.fori_loop(0, tiles, drain, 0)

        @pl.when(is_owner)
        def _(ch=ch):
            def drain_back(k, _):
                back_copy(lax.rem(chip + k, chips), ch).wait_send()
                return 0

            lax.fori_loop(1, chips, drain_back, 0)


def chain_peers(chips, chip, core):
    return [
        (chips - 1, lambda k: {"tm": 2 * lax.rem(chip + 1 + k, chips) + core}),
        (1, lambda k: {"tm": 2 * chip + 1 - core}),
    ]


def chain_scratch(chips, half, tiles):
    width, full = half // CHUNKS, tiles * ROWS
    wide = 2 * width + LANES
    f32 = jnp.float32
    dma = pltpu.SemaphoreType.DMA
    return [
        pltpu.VMEM((LANES, LANES), f32), pltpu.VMEM((LANES, LANES), f32),
        pltpu.VMEM((CHUNKS, full, wide), f32), pltpu.VMEM((CHUNKS, full, wide), f32),
        pltpu.VMEM((CHUNKS, full, 2 * width), f32),
        pltpu.VMEM((CHUNKS, full, wide), f32), pltpu.VMEM((CHUNKS, chips, ROWS, wide), f32),
        pltpu.VMEM((CHUNKS, chips, ROWS, 2 * width), f32), pltpu.VMEM((CHUNKS, full, 2 * width), f32),
        pltpu.VMEM((CHUNKS, full, 2 * width), f32), pltpu.VMEM((CHUNKS, full, 2 * width), f32),
        dma((CHUNKS,)), dma((CHUNKS,)), dma((CHUNKS, tiles)), dma((CHUNKS, chips)), dma((CHUNKS, chips)),
        dma((CHUNKS, tiles)), dma((CHUNKS, tiles)), dma((CHUNKS, tiles)),
    ]


def lanes_of(side, ch, half):
    width = half // CHUNKS
    return pl.ds(pl.multiple_of(side * half + ch * width, LANES), width)


def smooth_kernel(chips, x_hbm, decay_ref, gain_ref, norm_ref, doc_ref, word_ref, count_ref,
                  tw_ref, order_ref, edge_ref, raw, xs, load_sem, flat, table, spread, *bufs):
    core, chip = lax.rem(lax.axis_index("tm"), 2), lax.axis_index("tm") // 2
    slices, full, words = xs.shape
    half, tiles, blocks = words // 2, full // ROWS, words // LANES
    pitch = slices * blocks
    load = pltpu.make_async_copy(x_hbm, raw.at[0 : x_hbm.shape[0]], load_sem.at[0])
    load.start()
    decay = [decay_ref[s : s + 1, :] for s in range(2)]
    gain = [gain_ref[s : s + 1, :] for s in range(2)]
    norm = [norm_ref[s : s + 1, :] for s in range(2)]
    keep = keep_rows(gain_ref, slices * 2 * chips)
    one = jnp.ones_like(decay[0])
    spread_coefs(
        [decay[0], decay[1], one, 1.0 - decay[0], 1.0 - decay[1], gain[1], gain[0], one,
         keep[0], keep[1], norm[0], norm[1]], table, spread)
    if x_hbm.shape[0] < raw.shape[0]:
        raw[x_hbm.shape[0] :, :] = jnp.zeros((raw.shape[0] - x_hbm.shape[0], LANES), jnp.float32)
    greet(chain_peers(chips, chip, core))
    load.wait()

    def move(r, _):
        rows = pl.ds(pl.multiple_of(r * ROWS, ROWS), ROWS)
        for s in range(slices):
            for i in range(blocks):
                xs[s, rows, i * LANES : (i + 1) * LANES] = raw[
                    pl.ds(r * (ROWS * pitch) + i * slices + s, ROWS, stride=pitch), :]
        return 0

    lax.fori_loop(0, tiles, move, 0)

    def source(s, r, side, ch):
        return xs[s, pl.ds(pl.multiple_of(r * ROWS, ROWS), ROWS), lanes_of(side, ch, half)]

    def finish(s, r, side, ch, q):
        rows = pl.ds(pl.multiple_of(r * ROWS, ROWS), ROWS)
        tw_ref[s, rows, lanes_of(side, ch, half)] = jnp.exp(q - spread[rows, X0 + s : X0 + s + 1])

    def order():
        word = word_ref[...] - lax.axis_index("word") * words
        doc = doc_ref[...]
        keys = (((doc >> 8) * WORD_SPAN + word) << 12) | ((doc & 255) << 4) | count_ref[...]
        keys = sort_entries(keys)
        edge_ref[0:8, :] = keys[0:8]
        edge_ref[8:16, :] = keys[-8:]
        flat[...] = keys
        for s in range(slices):
            order_ref[s, 0:128, :] = flat[pl.ds(s, 128, stride=slices), :].T
            order_ref[s, 128:, :] = jnp.full((SPARE - 128, 128), -1, jnp.int32)

    two_sided(chips, chip, core, half, tiles, spread, source, finish, order, bufs)


def adjoint_kernel(chips, shares, e_hbm, t_hbm, tot_ref, sums_ref, decay_ref, gain_ref, out_ref, own_ref,
                   es, ts, load_sem, totals, tot_in, sums_in, tot_sem, sum_sem, table, spread, *bufs):
    core, chip = lax.rem(lax.axis_index("tm"), 2), lax.axis_index("tm") // 2
    share = lax.axis_index("word")
    slices, full, words = es.shape
    half, tiles, blocks = words // 2, full // ROWS, words // LANES
    pitch = slices * blocks
    loads = [pltpu.make_async_copy(e_hbm, es, load_sem.at[0]), pltpu.make_async_copy(t_hbm, ts, load_sem.at[1])]
    for load in loads:
        load.start()
    decay = [decay_ref[s : s + 1, :] for s in range(2)]
    gain = [gain_ref[s : s + 1, :] for s in range(2)]
    keep = keep_rows(gain_ref, slices * 2 * chips)
    one = jnp.ones_like(decay[0])
    spread_coefs(
        [one, gain[0], gain[1], one, one, one, decay[1], decay[0],
         keep[0], keep[1], 1.0 - decay[0], 1.0 - decay[1]], table, spread)
    neighbour = lambda k: {"word": lax.rem(share + 1 + k, shares)}
    greet(chain_peers(chips, chip, core) + [(shares - 1, neighbour)])

    def tot_copy(k):
        return pltpu.make_async_remote_copy(
            src_ref=tot_ref, dst_ref=tot_in.at[shares - 2 - k], send_sem=tot_sem.at[0, k],
            recv_sem=tot_sem.at[1, shares - 2 - k], device_id=neighbour(k), device_id_type=MESH)

    def sum_copy(k):
        return pltpu.make_async_remote_copy(
            src_ref=sums_ref.at[lax.rem(share + 1 + k, shares)], dst_ref=sums_in.at[shares - 2 - k],
            send_sem=sum_sem.at[0, k], recv_sem=sum_sem.at[1, shares - 2 - k],
            device_id=neighbour(k), device_id_type=MESH)

    for k in range(shares - 1):
        tot_copy(k).start()
    for k in range(shares - 1):
        sum_copy(k).start()
    for load in loads:
        load.wait()
    total = tot_ref[...]
    for k in range(shares - 1):
        tot_copy(shares - 2 - k).wait_recv()
        total = total + tot_in[k]
    totals[...] = total

    def source(s, r, side, ch):
        rows, lanes = pl.ds(pl.multiple_of(r * ROWS, ROWS), ROWS), lanes_of(side, ch, half)
        return es[s, rows, lanes] - totals[rows, s : s + 1] * ts[s, rows, lanes]

    def finish(s, r, side, ch, q):
        rows = pl.ds(pl.multiple_of(r * ROWS, ROWS), ROWS)
        grad = spread[rows, X0 + s : X0 + s + 1] * q
        width = half // CHUNKS
        at = r * (ROWS * pitch) + (side * half + ch * width) // LANES * slices + s
        for i in range(width // LANES):
            out_ref[pl.ds(at + i * slices, ROWS, stride=pitch), :] = grad[:, i * LANES : (i + 1) * LANES]

    def gather_sums():
        for s in range(slices):
            sums = sums_ref[share, s]
            for k in range(shares - 1):
                if s == 0:
                    sum_copy(shares - 2 - k).wait_recv()
                sums = sums + sums_in[k, s]
            own_ref[pl.ds(s, full, stride=slices), :] = sums

    two_sided(chips, chip, core, half, tiles, spread, source, finish, gather_sums, bufs)
    for k in range(shares - 1):
        tot_copy(k).wait_send()
        sum_copy(k).wait_send()


def sort_entries(x):
    shape = (x.shape[0] // 8, 8, 128)
    x = x.reshape(shape)
    high = shape[0].bit_length() - 1
    depth = high + 2 + 7
    sub = lax.broadcasted_iota(jnp.int32, (8, 128), 0)
    lane = lax.broadcasted_iota(jnp.int32, (8, 128), 1)

    def bit_of(j):
        return (sub >> (j - high + 1)) & 1 if j < high + 2 else (lane >> (j - high - 2)) & 1

    def parts(x, j):
        pieces = x.reshape((shape[0] >> (j + 1), 2, 1 << j, 8, 128))
        return pieces[:, 0], pieces[:, 1]

    def joined(a, b):
        return jnp.stack([a, b], axis=1).reshape(shape)

    def flip(x, k):
        if k >= depth:
            return x
        if k >= high:
            return x ^ (-bit_of(k))[None]
        a, b = parts(x, k)
        return joined(a, ~b)

    def exchange(x, j):
        if j < high:
            a, b = parts(x, j)
            return joined(jnp.minimum(a, b), jnp.maximum(a, b))
        low = (bit_of(j) == 0)[None]
        if j < high + 2:
            step, size = 1 << (j - high + 1), 8
            y = x
        else:
            step, size = 1 << (j - high - 2), 128
            y = x.reshape((shape[0] * 8, 128))
        partner = ahead = pltpu.roll(y, size - step, 1).reshape(shape)
        if 2 * step != size:
            partner = jnp.where(low, ahead, pltpu.roll(y, step, 1).reshape(shape))
        return jnp.where(low, jnp.minimum(x, partner), jnp.maximum(x, partner))

    for k in range(1, depth + 1):
        x = flip(x, k)
        for j in range(k - 1, -1, -1):
            x = exchange(x, j)
        x = flip(x, k)
    return x.reshape((shape[0] * 8, 128))


def tally_kernel(topics, tw_hbm, w_ref, order_ref, edge_ref, exp_hbm, tot_ref, sums_ref,
                 tws, exps, load_sem, save_sem, bounds, wraw, w32, wt, wb, tr, acc, ratio, sums, tots, place):
    slices, full, words = tws.shape
    shares = sums_ref.shape[0]
    docs = w32.shape[1]
    tiles, blocks, pieces = words // TILE_W, docs // TILE_D, docs // LANES

    def load(s):
        return pltpu.make_async_copy(tw_hbm.at[s], tws.at[s], load_sem.at[s])

    def save(s):
        return pltpu.make_async_copy(exps.at[s], exp_hbm.at[s], save_sem.at[s])

    for s in range(slices):
        load(s).start()
    for s in range(slices):
        least, most = edge_ref[s : s + 1, :], edge_ref[16 - slices + s : 17 - slices + s, :]
        for h in range(blocks):
            for j in range(tiles):
                low = (h * WORD_SPAN + j * TILE_W) << 12
                bounds[s, h, j, 0] = jnp.sum((most < low).astype(jnp.int32))
                bounds[s, h, j, 1] = jnp.sum((least < low + (TILE_W << 12)).astype(jnp.int32))

    wraw[w_ref.shape[0] :, :] = jnp.zeros((wraw.shape[0] - w_ref.shape[0], LANES), jnp.float32)
    wraw[0 : w_ref.shape[0], :] = w_ref[...].astype(jnp.float32)
    w32[...] = jnp.zeros_like(w32)
    tr[full // 16 * 16 :, :] = jnp.zeros((128 - full // 16 * 16, words), jnp.bfloat16)
    lane = lax.broadcasted_iota(jnp.int32, tot_ref.shape, 1)
    place[...] = lax.broadcasted_iota(jnp.int32, place.shape, 0).astype(jnp.float32).astype(jnp.bfloat16)
    pitch = slices * pieces

    def one_slice(s, _):
        for i in range(pieces):
            w32[0:full, i * LANES : (i + 1) * LANES] = wraw[pl.ds(i * slices + s, full, stride=pitch), :]
        wb[...] = w32[...].astype(jnp.bfloat16)
        wt[...] = w32[...].T.astype(jnp.bfloat16)
        load(s).wait()
        tr[0:full, :] = tws[s].astype(jnp.bfloat16)
        sums[...] = jnp.zeros_like(sums)
        tots[...] = jnp.zeros_like(tots)

        def one_tile(j, _):
            lanes = pl.ds(pl.multiple_of(j * TILE_W, TILE_W), TILE_W)
            topic = tr[:, lanes]
            acc[...] = jnp.zeros_like(acc)
            starts = [bounds[s, h, j, 0] for h in range(blocks)]
            longest = starts[0] * 0
            for h in range(blocks):
                longest = jnp.maximum(longest, (bounds[s, h, j, 1] - starts[h] + DEEP - 1) // DEEP)

            def batch(i, _):
                for h in range(blocks):
                    base = h * WORD_SPAN + j * TILE_W
                    at = jnp.minimum(starts[h] + DEEP * i, SPARE - DEEP)
                    key = jnp.concatenate(
                        [order_ref[s, pl.ds(at + n, 1), :] for n in range(DEEP)], axis=1)
                    word = ((key >> 12) - base).astype(jnp.float32).astype(jnp.bfloat16)
                    doc = ((key >> 4) & 255).astype(jnp.float32).astype(jnp.bfloat16)
                    count = (key & 15).astype(jnp.float32).astype(jnp.bfloat16)
                    docs_hot = jnp.where(place[...] == doc, count, jnp.bfloat16(0))
                    words_hot = jnp.where(place[...] == word, jnp.bfloat16(1), jnp.bfloat16(0))
                    acc[h] += lax.dot_general(
                        docs_hot, words_hot, (((1,), (1,)), ((), ())), preferred_element_type=jnp.float32)
                return 0

            lax.fori_loop(0, longest, batch, 0)
            for h in range(blocks):
                mixture = jnp.dot(
                    wt[h * TILE_D : (h + 1) * TILE_D, :], topic, preferred_element_type=jnp.float32)
                ratio[h * TILE_D : (h + 1) * TILE_D, :] = (acc[h] / mixture).astype(jnp.bfloat16)
            sums[...] += lax.dot_general(
                topic, ratio[...], (((1,), (1,)), ((), ())), preferred_element_type=jnp.float32)
            weighted = jnp.dot(wb[...], ratio[...], preferred_element_type=jnp.float32)
            expected = topic[0:full].astype(jnp.float32) * weighted[0:full]
            exps[s, :, lanes] = expected
            tots[...] += expected
            return 0

        lax.fori_loop(0, tiles, one_tile, 0)
        save(s).start()
        for y in range(shares):
            own = slice(y * (docs // shares), (y + 1) * (docs // shares))
            sums_ref[y, s] = sums[0:full, own] * w32[0:full, own]
        total = jnp.sum(tots[...], axis=1, keepdims=True)
        tot_ref[...] = jnp.where(lane == s, total, jnp.where(s == 0, 0.0, tot_ref[...]))
        return 0

    lax.fori_loop(0, slices, one_slice, 0)
    for s in range(slices):
        save(s).wait()


VMEM_SPEC = pl.BlockSpec(memory_space=pltpu.VMEM)
ANY_SPEC = pl.BlockSpec(memory_space=pl.ANY)
LIMIT = 60 * 1024 * 1024


def tally(topic_word, weights, order, edges, topics, shares):
    slices, full, words = topic_word.shape
    docs = weights.shape[0] * LANES // (slices * topics)
    f32, bf16 = jnp.float32, jnp.bfloat16
    dma = pltpu.SemaphoreType.DMA
    return pl.pallas_call(
        functools.partial(tally_kernel, topics),
        out_shape=(
            jax.ShapeDtypeStruct((slices, full, words), f32),
            jax.ShapeDtypeStruct((full, LANES), f32),
            jax.ShapeDtypeStruct((shares, slices, full, docs // shares), f32),
        ),
        in_specs=[ANY_SPEC] + [VMEM_SPEC] * 3,
        out_specs=(ANY_SPEC, VMEM_SPEC, VMEM_SPEC),
        scratch_shapes=[
            pltpu.VMEM((slices, full, words), f32), pltpu.VMEM((slices, full, words), f32),
            dma((slices,)), dma((slices,)),
            pltpu.SMEM((slices, docs // TILE_D, words // TILE_W, 2), jnp.int32),
            pltpu.VMEM((full * slices * docs // LANES, LANES), f32),
            pltpu.VMEM((128, docs), f32), pltpu.VMEM((docs, 128), bf16), pltpu.VMEM((128, docs), bf16),
            pltpu.VMEM((128, words), bf16), pltpu.VMEM((docs // TILE_D, TILE_D, TILE_W), f32),
            pltpu.VMEM((docs, TILE_W), bf16), pltpu.VMEM((128, docs), f32), pltpu.VMEM((full, TILE_W), f32),
            pltpu.VMEM((TILE_W, DEEP * 128), bf16),
        ],
        compiler_params=pltpu.CompilerParams(vmem_limit_bytes=LIMIT),
        name="tally",
    )(topic_word, weights, order, edges)


def interleaved(x):
    slices, rows, columns = x.shape
    group = 4 if columns % (4 * LANES) == 0 else 1
    x = x.transpose((1, 0, 2)).reshape((rows, slices, columns // LANES // group, group, LANES))
    x = x.transpose((0, 2, 3, 1, 4))
    return x.reshape((rows * columns // LANES * slices, LANES))


def separated(x, slices, rows, columns):
    x = x[: rows * columns // LANES * slices].reshape((rows, columns // LANES, slices, LANES))
    return x.transpose((0, 2, 1, 3)).reshape((rows, slices, columns)).transpose((1, 0, 2))


def make_local(chips, shares):
    def local(pseudo_obs, filter_decay, smooth_gain, log_norm, doc_weights, doc_ids, word_ids, counts):
        slices, topics, words = pseudo_obs.shape
        tiles, half = -(-topics // ROWS), words // 2
        full = tiles * ROWS
        docs = doc_weights.shape[2]
        entries = doc_ids.shape[1]
        f32 = jnp.float32
        dma = pltpu.SemaphoreType.DMA
        flat_rows = full * slices * words // LANES
        ids = [interleaved(a[:, None, :]) for a in (doc_ids, word_ids, counts)]
        topic_word, order, edges = pl.pallas_call(
            functools.partial(smooth_kernel, chips),
            out_shape=(
                jax.ShapeDtypeStruct((slices, full, words), f32),
                jax.ShapeDtypeStruct((slices, SPARE, LANES), jnp.int32),
                jax.ShapeDtypeStruct((16, LANES), jnp.int32),
            ),
            in_specs=[ANY_SPEC] + [VMEM_SPEC] * 6,
            out_specs=(VMEM_SPEC,) * 3,
            scratch_shapes=[
                pltpu.VMEM((flat_rows, LANES), f32), pltpu.VMEM((slices, full, words), f32), dma((1,)),
                pltpu.VMEM((slices * entries // LANES, LANES), jnp.int32),
            ] + chain_scratch(chips, half, tiles),
            compiler_params=pltpu.CompilerParams(
                collective_id=0, has_side_effects=True, vmem_limit_bytes=LIMIT),
            name="smooth",
        )(interleaved(pseudo_obs), filter_decay, smooth_gain, log_norm, *ids)
        expected, totals, sums = tally(topic_word, interleaved(doc_weights), order, edges, topics, shares)
        grad, own = pl.pallas_call(
            functools.partial(adjoint_kernel, chips, shares),
            out_shape=(
                jax.ShapeDtypeStruct((flat_rows, LANES), f32),
                jax.ShapeDtypeStruct((slices * full, docs // shares), f32),
            ),
            in_specs=[ANY_SPEC, ANY_SPEC] + [VMEM_SPEC] * 4,
            out_specs=(VMEM_SPEC, VMEM_SPEC),
            scratch_shapes=[
                pltpu.VMEM((slices, full, words), f32), pltpu.VMEM((slices, full, words), f32), dma((2,)),
                pltpu.VMEM((full, LANES), f32), pltpu.VMEM((shares - 1, full, LANES), f32),
                pltpu.VMEM((shares - 1, slices, full, docs // shares), f32),
                dma((2, shares - 1)), dma((2, shares - 1)),
            ] + chain_scratch(chips, half, tiles),
            compiler_params=pltpu.CompilerParams(
                collective_id=1, has_side_effects=True, vmem_limit_bytes=LIMIT),
            name="adjoint",
        )(expected, topic_word, totals, sums, filter_decay, smooth_gain)
        return separated(grad, slices, topics, words), separated(own, slices, topics, docs // shares)

    return local


def solution(mesh):
    return jax.shard_map(
        make_local(mesh.shape["tm"] // 2, mesh.shape["word"]),
        mesh=mesh,
        in_specs=(
            P("tm", None, "word"),
            P("tm", None),
            P("tm", None),
            P("tm", None),
            P("tm", None, None),
            P("tm", "word"),
            P("tm", "word"),
            P("tm", "word"),
        ),
        out_specs=(P("tm", None, "word"), P("tm", None, "word")),
        check_vma=False,
    )
```

time: 196 us -> 146 us (0.74)
  Pallas kernels: 177 us -> 141 us
  local copies, waits for them, and re-layouts: 14.1 us -> 3.69 us
  other arithmetic: 4.03 us -> 0 us
    pallas_call x1, Pallas kernels: 57 us -> 28.1 us  [tally(): pl.pallas_call(functools.partial(tally_kernel, topics), out_shape=(jax.Sh...]
    unnamed x5 -> x2, local copies, waits for them, and re-layouts: 10.8 us -> 0.01 us
    pallas_call x1, Pallas kernels: 62.7 us -> 57.2 us  [local(): pl.pallas_call(functools.partial(adjoint_kernel, chips, shares), out_shap...]
    slice x0 -> x2, local copies, waits for them, and re-layouts: none -> 3.69 us  [separated(): x[:rows * columns // LANES * slices]]
    concatenate x2 -> x0, local copies, waits for them, and re-layouts: 2.11 us -> none  [coef_rows(): table = jnp.concatenate([r[None] for r in rows], axis=0)]
where the time goes in v2:
time: 146 us; the launch traced here: 145 us
  Pallas kernels  141 us (97%)
  local copies, waits for them, and re-layouts  3.69 us (3%)
    pallas_call x1, Pallas kernels, local(): pl.pallas_call(functools.partial(adjoint_kernel, chips, shares), out_shap...  57.2 us
    pallas_call x1, Pallas kernels, local(): pl.pallas_call(functools.partial(smooth_kernel, chips), out_shape=(jax.Sh...  55.6 us
    pallas_call x1, Pallas kernels, tally(): pl.pallas_call(functools.partial(tally_kernel, topics), out_shape=(jax.Sh...  28.1 us
    slice x2, local copies, waits for them, and re-layouts, separated(): x[:rows * columns // LANES * slices]  3.69 us

profile of v2, /device:TPU:1, one launch (start us, length us, event | category | flops | bytes accessed | tf_op | source)
XLA Modules:
  0.0 145.4 jit_solution(16584155291029519221)
XLA Ops:
  0.6 55.6 %smooth.1 = (f32[2,104,2560]{2,1,0:T(8,128)}, s32[2,136,128]{2,1,0:T(8,128)}, s32[16,128]{1,0:T(8,128)}) custom-call(f32[4000,128]{1,0:T(8,128)} %bitcast.39, f32[2,100]{1,0:T(2,128)} %decay_ref.3, f32[2,100]{1,0:T(2,128)} %gain_ref.3, f32[2,100]{1,0:T(2,128)} %norm_ref.1, s32[256,128]{1,0:T(8,128)} %bitcast.42, s32[256,128]{1,0:T(8,128)} %bitcast.43, ...), custom_call_target="tpu_custom_call" | custom-call | tf_op jit(solution)/shard_map/smooth/pallas_call | solution.py:621
  56.3 28.1 %tally.1 = (f32[2,104,2560]{2,1,0:T(8,128)}, f32[104,128]{1,0:T(8,128)}, f32[4,2,104,128]{3,2,1,0:T(8,128)}) custom-call(f32[2,104,2560]{2,1,0:T(8,128)} %get-tuple-element.10.tw_hbm.t_hbm, bf16[800,128]{1,0:T(8,128)(2,1)} %bitcast.41, s32[2,136,128]{2,1,0:T(8,128)} %get-tuple-element.11.order_ref, s32[16,128]{1,0:T(8,128)} %get-tuple-element.12.edge_ref), custom_call_target="tpu_custom_call" | custom-call | tf_op jit(solution)/shard_map/tally/pallas_call | solution.py:573
  84.4 57.2 %adjoint.1 = (f32[4160,128]{1,0:T(8,128)}, f32[208,128]{1,0:T(8,128)}) custom-call(f32[2,104,2560]{2,1,0:T(8,128)} %get-tuple-element.13.e_hbm, f32[2,104,2560]{2,1,0:T(8,128)} %get-tuple-element.10.tw_hbm.t_hbm, f32[104,128]{1,0:T(8,128)} %get-tuple-element.14.tot_ref, f32[4,2,104,128]{3,2,1,0:T(8,128)} %get-tuple-element.15.sums_ref, f32[2,100]{1,0:T(2,128)} %decay_ref.3, ...), custom_call_target="tpu_custom_call" | custom-call | tf_op jit(solution)/shard_map/adjoint/pallas_call | solution.py:639
  141.7 0.0 copy-start
  141.7 3.0 %slice.6 = f32[4000,128]{1,0:T(8,128)} slice(f32[4160,128]{1,0:T(8,128)} %get-tuple-element.16), slice={[0:4000], [0:128]} | slice | bytes 4096000 | tf_op jit(solution)/shard_map/slice | solution.py:606
  144.7 0.0 copy-done
  144.7 0.6 slice.7
Async XLA Ops:
  141.7 3.1 %copy-start = (f32[208,128]{1,0:T(8,128)S(1)}, f32[208,128]{1,0:T(8,128)}, u32[]{:S(2)}) copy-start(f32[208,128]{1,0:T(8,128)} %get-tuple-element.17) | copy-start | bytes 319492

commit v3 on v2

--- a/solution.py
+++ b/solution.py
@@ -15,6 +15,7 @@
 WORD_SPAN = 4096
 SPARE = 136
 DEEP = 4
+TOGETHER = 2
 CHUNKS = 2
 M_IN, A1, M_OUT, B0, B1, N_IN, C0, N_OUT, E0, E1, X0, X1, DEV_D, DEV_G, DEV_Q = range(15)
 
@@ -26,7 +27,7 @@
             pl.semaphore_signal(barrier, inc=1, device_id=peer(k), device_id_type=MESH)
             return 0
         lax.fori_loop(0, count, hello, 0)
-    pl.semaphore_wait(barrier, sum(count for count, _ in peers))
+    return lambda: pl.semaphore_wait(barrier, sum(count for count, _ in peers))
 
 
 def spread_coefs(rows, table, spread):
@@ -56,7 +57,7 @@
     return lambda r: r, lambda c: c, lambda c: c < tiles
 
 
-def two_sided(chips, chip, core, half, tiles, spread, source, finish, meanwhile, bufs):
+def two_sided(chips, chip, core, half, tiles, spread, source, finish, meanwhile, meet, bufs):
     (psend, precv, mine, cbuf, rbuf, obuf, wbuf, gsend, grecv,
      pair_send, pair_recv, out_send, out_recv, back_send, back_recv, give_send, give_recv) = bufs
     first = core == 0
@@ -97,6 +98,8 @@
             return 0
 
         lax.fori_loop(0, tiles, give_ends, 0)
+        if ch == 0 and meet is not None:
+            meet()
         swap(ch).start()
 
     for ch in range(CHUNKS):
@@ -234,7 +237,6 @@
 
         lax.fori_loop(0, tiles, own_half, 0)
 
-    for ch in range(CHUNKS):
         def other_half(k, _, ch=ch):
             r = turn(k)
             give_copy(r, ch).wait_recv()
@@ -301,6 +303,7 @@
     slices, full, words = xs.shape
     half, tiles, blocks = words // 2, full // ROWS, words // LANES
     pitch = slices * blocks
+    meet = greet(chain_peers(chips, chip, core))
     load = pltpu.make_async_copy(x_hbm, raw.at[0 : x_hbm.shape[0]], load_sem.at[0])
     load.start()
     decay = [decay_ref[s : s + 1, :] for s in range(2)]
@@ -313,7 +316,6 @@
          keep[0], keep[1], norm[0], norm[1]], table, spread)
     if x_hbm.shape[0] < raw.shape[0]:
         raw[x_hbm.shape[0] :, :] = jnp.zeros((raw.shape[0] - x_hbm.shape[0], LANES), jnp.float32)
-    greet(chain_peers(chips, chip, core))
     load.wait()
 
     def move(r, _):
@@ -345,19 +347,21 @@
             order_ref[s, 0:128, :] = flat[pl.ds(s, 128, stride=slices), :].T
             order_ref[s, 128:, :] = jnp.full((SPARE - 128, 128), -1, jnp.int32)
 
-    two_sided(chips, chip, core, half, tiles, spread, source, finish, order, bufs)
-
-
-def adjoint_kernel(chips, shares, e_hbm, t_hbm, tot_ref, sums_ref, decay_ref, gain_ref, out_ref, own_ref,
-                   es, ts, load_sem, totals, tot_in, sums_in, tot_sem, sum_sem, table, spread, *bufs):
+    two_sided(chips, chip, core, half, tiles, spread, source, finish, order, meet, bufs)
+
+
+def adjoint_kernel(chips, shares, t_hbm, dense_hbm, w_ref, decay_ref, gain_ref, out_ref, own_ref,
+                   es, ts, tot_ref, sums_ref, load_sem, dense, dense_sem, wraw, w32, wb, wt, tr, ratio, sums, tots,
+                   totals, tot_in, sums_in, tot_sem, sum_sem, table, spread, *bufs):
     core, chip = lax.rem(lax.axis_index("tm"), 2), lax.axis_index("tm") // 2
     share = lax.axis_index("word")
     slices, full, words = es.shape
     half, tiles, blocks = words // 2, full // ROWS, words // LANES
     pitch = slices * blocks
-    loads = [pltpu.make_async_copy(e_hbm, es, load_sem.at[0]), pltpu.make_async_copy(t_hbm, ts, load_sem.at[1])]
-    for load in loads:
-        load.start()
+    neighbour = lambda k: {"word": lax.rem(share + 1 + k, shares)}
+    meet = greet(chain_peers(chips, chip, core) + [(shares - 1, neighbour)])
+    expect(t_hbm, dense_hbm, w_ref, es, ts, tot_ref, sums_ref, load_sem, dense, dense_sem,
+           wraw, w32, wb, wt, tr, ratio, sums, tots)
     decay = [decay_ref[s : s + 1, :] for s in range(2)]
     gain = [gain_ref[s : s + 1, :] for s in range(2)]
     keep = keep_rows(gain_ref, slices * 2 * chips)
@@ -365,8 +369,7 @@
     spread_coefs(
         [one, gain[0], gain[1], one, one, one, decay[1], decay[0],
          keep[0], keep[1], 1.0 - decay[0], 1.0 - decay[1]], table, spread)
-    neighbour = lambda k: {"word": lax.rem(share + 1 + k, shares)}
-    greet(chain_peers(chips, chip, core) + [(shares - 1, neighbour)])
+    meet()
 
     def tot_copy(k):
         return pltpu.make_async_remote_copy(
@@ -383,8 +386,6 @@
         tot_copy(k).start()
     for k in range(shares - 1):
         sum_copy(k).start()
-    for load in loads:
-        load.wait()
     total = tot_ref[...]
     for k in range(shares - 1):
         tot_copy(shares - 2 - k).wait_recv()
@@ -412,7 +413,7 @@
                 sums = sums + sums_in[k, s]
             own_ref[pl.ds(s, full, stride=slices), :] = sums
 
-    two_sided(chips, chip, core, half, tiles, spread, source, finish, gather_sums, bufs)
+    two_sided(chips, chip, core, half, tiles, spread, source, finish, gather_sums, None, bufs)
     for k in range(shares - 1):
         tot_copy(k).wait_send()
         sum_copy(k).wait_send()
@@ -468,96 +469,128 @@
     return x.reshape((shape[0] * 8, 128))
 
 
-def tally_kernel(topics, tw_hbm, w_ref, order_ref, edge_ref, exp_hbm, tot_ref, sums_ref,
-                 tws, exps, load_sem, save_sem, bounds, wraw, w32, wt, wb, tr, acc, ratio, sums, tots, place):
-    slices, full, words = tws.shape
-    shares = sums_ref.shape[0]
-    docs = w32.shape[1]
-    tiles, blocks, pieces = words // TILE_W, docs // TILE_D, docs // LANES
-
-    def load(s):
-        return pltpu.make_async_copy(tw_hbm.at[s], tws.at[s], load_sem.at[s])
-
-    def save(s):
-        return pltpu.make_async_copy(exps.at[s], exp_hbm.at[s], save_sem.at[s])
-
-    for s in range(slices):
-        load(s).start()
+def count_kernel(words, order_ref, edge_ref, dense_hbm, bounds, place, acc, save_sem):
+    slices = order_ref.shape[0]
+    tiles, blocks = words // TILE_W, acc.shape[1] // TILE_D
+    together = acc.shape[0] // 2
     for s in range(slices):
         least, most = edge_ref[s : s + 1, :], edge_ref[16 - slices + s : 17 - slices + s, :]
         for h in range(blocks):
             for j in range(tiles):
                 low = (h * WORD_SPAN + j * TILE_W) << 12
-                bounds[s, h, j, 0] = jnp.sum((most < low).astype(jnp.int32))
-                bounds[s, h, j, 1] = jnp.sum((least < low + (TILE_W << 12)).astype(jnp.int32))
-
+                bounds[s * tiles + j, h, 0] = jnp.sum((most < low).astype(jnp.int32))
+                bounds[s * tiles + j, h, 1] = jnp.sum((least < low + (TILE_W << 12)).astype(jnp.int32))
+    place[...] = lax.broadcasted_iota(jnp.int32, place.shape, 0).astype(jnp.float32).astype(jnp.bfloat16)
+
+    def save(t, slot):
+        return pltpu.make_async_copy(
+            acc.at[pl.ds(slot * together, together)], dense_hbm.at[pl.ds(t * together, together)], save_sem.at[slot])
+
+    def step(t, _):
+        slot = lax.rem(t, 2)
+        s = lax.div(t * together, tiles)
+
+        @pl.when(t >= 2)
+        def _():
+            save(t - 2, slot).wait()
+
+        acc[pl.ds(slot * together, together)] = jnp.zeros((together,) + acc.shape[1:], jnp.float32)
+        groups = [(n, h) for n in range(together) for h in range(blocks)]
+        starts = [bounds[t * together + n, h, 0] for n, h in groups]
+        longest = starts[0] * 0
+        for start, (n, h) in zip(starts, groups):
+            longest = jnp.maximum(longest, (bounds[t * together + n, h, 1] - start + DEEP - 1) // DEEP)
+
+        def batch(i, _):
+            for start, (n, h) in zip(starts, groups):
+                base = h * WORD_SPAN + (t * together + n - s * tiles) * TILE_W
+                at = jnp.minimum(start + DEEP * i, SPARE - DEEP)
+                key = jnp.concatenate([order_ref[s, pl.ds(at + m, 1), :] for m in range(DEEP)], axis=1)
+                word = ((key >> 12) - base).astype(jnp.float32).astype(jnp.bfloat16)
+                doc = ((key >> 4) & 255).astype(jnp.float32).astype(jnp.bfloat16)
+                count = (key & 15).astype(jnp.float32).astype(jnp.bfloat16)
+                docs_hot = jnp.where(place[...] == doc, count, jnp.bfloat16(0))
+                words_hot = jnp.where(place[...] == word, jnp.bfloat16(1), jnp.bfloat16(0))
+                acc[slot * together + n, h * TILE_D : (h + 1) * TILE_D, :] += lax.dot_general(
+                    docs_hot, words_hot, (((1,), (1,)), ((), ())), preferred_element_type=jnp.float32)
+            return 0
+
+        lax.fori_loop(0, longest, batch, 0)
+        save(t, slot).start()
+        return 0
+
+    steps = slices * tiles // together
+    lax.fori_loop(0, steps, step, 0)
+    for t in (steps - 2, steps - 1):
+        save(t, t % 2).wait()
+
+
+def fill_slice(s, wraw, w32, wb, wt):
+    slices, pieces = 2, w32.shape[1] // LANES
+    full = wraw.shape[0] // (slices * pieces)
+    for i in range(pieces):
+        w32[0:full, i * LANES : (i + 1) * LANES] = wraw[pl.ds(i * slices + s, full, stride=slices * pieces), :]
+    wb[...] = w32[...].astype(jnp.bfloat16)
+    wt[...] = w32[...].T.astype(jnp.bfloat16)
+
+
+def expect(t_hbm, dense_hbm, w_ref, es, ts, tot, sums_out, load_sem, dense, dense_sem,
+           wraw, w32, wb, wt, tr, ratio, sums, tots):
+    slices, full, words = ts.shape
+    shares, docs = sums_out.shape[0], w32.shape[1]
+    tiles, blocks = words // TILE_W, docs // TILE_D
+
+    def load(s):
+        return pltpu.make_async_copy(t_hbm.at[s], ts.at[s], load_sem.at[s])
+
+    def fetch(t):
+        slot = lax.rem(t, 2)
+        return pltpu.make_async_copy(dense_hbm.at[t], dense.at[slot], dense_sem.at[slot])
+
+    for s in range(slices):
+        load(s).start()
+    fetch(0).start()
     wraw[w_ref.shape[0] :, :] = jnp.zeros((wraw.shape[0] - w_ref.shape[0], LANES), jnp.float32)
     wraw[0 : w_ref.shape[0], :] = w_ref[...].astype(jnp.float32)
     w32[...] = jnp.zeros_like(w32)
     tr[full // 16 * 16 :, :] = jnp.zeros((128 - full // 16 * 16, words), jnp.bfloat16)
-    lane = lax.broadcasted_iota(jnp.int32, tot_ref.shape, 1)
-    place[...] = lax.broadcasted_iota(jnp.int32, place.shape, 0).astype(jnp.float32).astype(jnp.bfloat16)
-    pitch = slices * pieces
-
-    def one_slice(s, _):
-        for i in range(pieces):
-            w32[0:full, i * LANES : (i + 1) * LANES] = wraw[pl.ds(i * slices + s, full, stride=pitch), :]
-        wb[...] = w32[...].astype(jnp.bfloat16)
-        wt[...] = w32[...].T.astype(jnp.bfloat16)
+    lane = lax.broadcasted_iota(jnp.int32, tot.shape, 1)
+    tot[...] = jnp.zeros_like(tot)
+
+    for s in range(slices):
+        fill_slice(s, wraw, w32, wb, wt)
         load(s).wait()
-        tr[0:full, :] = tws[s].astype(jnp.bfloat16)
+        tr[0:full, :] = ts[s].astype(jnp.bfloat16)
         sums[...] = jnp.zeros_like(sums)
         tots[...] = jnp.zeros_like(tots)
 
-        def one_tile(j, _):
+        def one_tile(j, _, s=s):
             lanes = pl.ds(pl.multiple_of(j * TILE_W, TILE_W), TILE_W)
             topic = tr[:, lanes]
-            acc[...] = jnp.zeros_like(acc)
-            starts = [bounds[s, h, j, 0] for h in range(blocks)]
-            longest = starts[0] * 0
+            t = s * tiles + j
+            fetch(t).wait()
+
+            @pl.when(t + 1 < slices * tiles)
+            def _():
+                fetch(t + 1).start()
+
             for h in range(blocks):
-                longest = jnp.maximum(longest, (bounds[s, h, j, 1] - starts[h] + DEEP - 1) // DEEP)
-
-            def batch(i, _):
-                for h in range(blocks):
-                    base = h * WORD_SPAN + j * TILE_W
-                    at = jnp.minimum(starts[h] + DEEP * i, SPARE - DEEP)
-                    key = jnp.concatenate(
-                        [order_ref[s, pl.ds(at + n, 1), :] for n in range(DEEP)], axis=1)
-                    word = ((key >> 12) - base).astype(jnp.float32).astype(jnp.bfloat16)
-                    doc = ((key >> 4) & 255).astype(jnp.float32).astype(jnp.bfloat16)
-                    count = (key & 15).astype(jnp.float32).astype(jnp.bfloat16)
-                    docs_hot = jnp.where(place[...] == doc, count, jnp.bfloat16(0))
-                    words_hot = jnp.where(place[...] == word, jnp.bfloat16(1), jnp.bfloat16(0))
-                    acc[h] += lax.dot_general(
-                        docs_hot, words_hot, (((1,), (1,)), ((), ())), preferred_element_type=jnp.float32)
-                return 0
-
-            lax.fori_loop(0, longest, batch, 0)
-            for h in range(blocks):
-                mixture = jnp.dot(
-                    wt[h * TILE_D : (h + 1) * TILE_D, :], topic, preferred_element_type=jnp.float32)
-                ratio[h * TILE_D : (h + 1) * TILE_D, :] = (acc[h] / mixture).astype(jnp.bfloat16)
+                rows = slice(h * TILE_D, (h + 1) * TILE_D)
+                mixture = jnp.dot(wt[rows, :], topic, preferred_element_type=jnp.float32)
+                ratio[rows, :] = (dense[lax.rem(t, 2), rows, :] / mixture).astype(jnp.bfloat16)
             sums[...] += lax.dot_general(
                 topic, ratio[...], (((1,), (1,)), ((), ())), preferred_element_type=jnp.float32)
             weighted = jnp.dot(wb[...], ratio[...], preferred_element_type=jnp.float32)
             expected = topic[0:full].astype(jnp.float32) * weighted[0:full]
-            exps[s, :, lanes] = expected
+            es[s, :, lanes] = expected
             tots[...] += expected
             return 0
 
         lax.fori_loop(0, tiles, one_tile, 0)
-        save(s).start()
         for y in range(shares):
             own = slice(y * (docs // shares), (y + 1) * (docs // shares))
-            sums_ref[y, s] = sums[0:full, own] * w32[0:full, own]
-        total = jnp.sum(tots[...], axis=1, keepdims=True)
-        tot_ref[...] = jnp.where(lane == s, total, jnp.where(s == 0, 0.0, tot_ref[...]))
-        return 0
-
-    lax.fori_loop(0, slices, one_slice, 0)
-    for s in range(slices):
-        save(s).wait()
+            sums_out[y, s] = sums[0:full, own] * w32[0:full, own]
+        tot[...] = jnp.where(lane == s, jnp.sum(tots[...], axis=1, keepdims=True), tot[...])
 
 
 VMEM_SPEC = pl.BlockSpec(memory_space=pltpu.VMEM)
@@ -565,33 +598,23 @@
 LIMIT = 60 * 1024 * 1024
 
 
-def tally(topic_word, weights, order, edges, topics, shares):
-    slices, full, words = topic_word.shape
-    docs = weights.shape[0] * LANES // (slices * topics)
-    f32, bf16 = jnp.float32, jnp.bfloat16
-    dma = pltpu.SemaphoreType.DMA
+def count_entries(order, edges, words, docs):
+    slices = order.shape[0]
+    tiles = words // TILE_W
     return pl.pallas_call(
-        functools.partial(tally_kernel, topics),
-        out_shape=(
-            jax.ShapeDtypeStruct((slices, full, words), f32),
-            jax.ShapeDtypeStruct((full, LANES), f32),
-            jax.ShapeDtypeStruct((shares, slices, full, docs // shares), f32),
-        ),
-        in_specs=[ANY_SPEC] + [VMEM_SPEC] * 3,
-        out_specs=(ANY_SPEC, VMEM_SPEC, VMEM_SPEC),
+        functools.partial(count_kernel, words),
+        out_shape=jax.ShapeDtypeStruct((slices * tiles, docs, TILE_W), jnp.float32),
+        in_specs=[VMEM_SPEC] * 2,
+        out_specs=ANY_SPEC,
         scratch_shapes=[
-            pltpu.VMEM((slices, full, words), f32), pltpu.VMEM((slices, full, words), f32),
-            dma((slices,)), dma((slices,)),
-            pltpu.SMEM((slices, docs // TILE_D, words // TILE_W, 2), jnp.int32),
-            pltpu.VMEM((full * slices * docs // LANES, LANES), f32),
-            pltpu.VMEM((128, docs), f32), pltpu.VMEM((docs, 128), bf16), pltpu.VMEM((128, docs), bf16),
-            pltpu.VMEM((128, words), bf16), pltpu.VMEM((docs // TILE_D, TILE_D, TILE_W), f32),
-            pltpu.VMEM((docs, TILE_W), bf16), pltpu.VMEM((128, docs), f32), pltpu.VMEM((full, TILE_W), f32),
-            pltpu.VMEM((TILE_W, DEEP * 128), bf16),
+            pltpu.SMEM((slices * tiles, docs // TILE_D, 2), jnp.int32),
+            pltpu.VMEM((TILE_W, DEEP * 128), jnp.bfloat16),
+            pltpu.VMEM((2 * TOGETHER, docs, TILE_W), jnp.float32),
+            pltpu.SemaphoreType.DMA((2,)),
         ],
         compiler_params=pltpu.CompilerParams(vmem_limit_bytes=LIMIT),
-        name="tally",
-    )(topic_word, weights, order, edges)
+        name="count",
+    )(order, edges)
 
 
 def interleaved(x):
@@ -614,7 +637,7 @@
         full = tiles * ROWS
         docs = doc_weights.shape[2]
         entries = doc_ids.shape[1]
-        f32 = jnp.float32
+        f32, bf16 = jnp.float32, jnp.bfloat16
         dma = pltpu.SemaphoreType.DMA
         flat_rows = full * slices * words // LANES
         ids = [interleaved(a[:, None, :]) for a in (doc_ids, word_ids, counts)]
@@ -635,17 +658,22 @@
                 collective_id=0, has_side_effects=True, vmem_limit_bytes=LIMIT),
             name="smooth",
         )(interleaved(pseudo_obs), filter_decay, smooth_gain, log_norm, *ids)
-        expected, totals, sums = tally(topic_word, interleaved(doc_weights), order, edges, topics, shares)
+        dense = count_entries(order, edges, words, docs)
         grad, own = pl.pallas_call(
             functools.partial(adjoint_kernel, chips, shares),
             out_shape=(
                 jax.ShapeDtypeStruct((flat_rows, LANES), f32),
                 jax.ShapeDtypeStruct((slices * full, docs // shares), f32),
             ),
-            in_specs=[ANY_SPEC, ANY_SPEC] + [VMEM_SPEC] * 4,
+            in_specs=[ANY_SPEC, ANY_SPEC] + [VMEM_SPEC] * 3,
             out_specs=(VMEM_SPEC, VMEM_SPEC),
             scratch_shapes=[
-                pltpu.VMEM((slices, full, words), f32), pltpu.VMEM((slices, full, words), f32), dma((2,)),
+                pltpu.VMEM((slices, full, words), f32), pltpu.VMEM((slices, full, words), f32),
+                pltpu.VMEM((full, LANES), f32), pltpu.VMEM((shares, slices, full, docs // shares), f32),
+                dma((slices,)), pltpu.VMEM((2, docs, TILE_W), f32), dma((2,)),
+                pltpu.VMEM((full * slices * docs // LANES, LANES), f32), pltpu.VMEM((128, docs), f32),
+                pltpu.VMEM((128, docs), bf16), pltpu.VMEM((docs, 128), bf16), pltpu.VMEM((128, words), bf16),
+                pltpu.VMEM((docs, TILE_W), bf16), pltpu.VMEM((128, docs), f32), pltpu.VMEM((full, TILE_W), f32),
                 pltpu.VMEM((full, LANES), f32), pltpu.VMEM((shares - 1, full, LANES), f32),
                 pltpu.VMEM((shares - 1, slices, full, docs // shares), f32),
                 dma((2, shares - 1)), dma((2, shares - 1)),
@@ -653,7 +681,7 @@
             compiler_params=pltpu.CompilerParams(
                 collective_id=1, has_side_effects=True, vmem_limit_bytes=LIMIT),
             name="adjoint",
-        )(expected, topic_word, totals, sums, filter_decay, smooth_gain)
+        )(topic_word, dense, interleaved(doc_weights), filter_decay, smooth_gain)
         return separated(grad, slices, topics, words), separated(own, slices, topics, docs // shares)
 
     return local

time: 146 us -> 151 us (1.034)
  Pallas kernels: 141 us -> 146 us
    pallas_call x1, Pallas kernels: 57.2 us -> 79 us  [local(): pl.pallas_call(functools.partial(adjoint_kernel, chips, shares), out_shap...]
    pallas_call x1, Pallas kernels: 28.1 us -> 12.9 us  [count_entries(): pl.pallas_call(functools.partial(count_kernel, words), out_shape=jax.Shap...]
    pallas_call x1, Pallas kernels: 55.6 us -> 53.9 us  [local(): pl.pallas_call(functools.partial(smooth_kernel, chips), out_shape=(jax.Sh...]
where the time goes in v3:
time: 151 us; the launch traced here: 150 us
  Pallas kernels  146 us (97%)
  local copies, waits for them, and re-layouts  3.69 us (2%)
    pallas_call x1, Pallas kernels, local(): pl.pallas_call(functools.partial(adjoint_kernel, chips, shares), out_shap...  79 us
    pallas_call x1, Pallas kernels, local(): pl.pallas_call(functools.partial(smooth_kernel, chips), out_shape=(jax.Sh...  53.9 us
    pallas_call x1, Pallas kernels, count_entries(): pl.pallas_call(functools.partial(count_kernel, words), out_shape=jax.Shap...  12.9 us
    slice x2, local copies, waits for them, and re-layouts, separated(): x[:rows * columns // LANES * slices]  3.69 us

profile of v3, /device:TPU:1, one launch (start us, length us, event | category | flops | bytes accessed | tf_op | source)
XLA Modules:
  0.0 150.2 jit_solution(1618248068668856678)
XLA Ops:
  0.6 53.9 %smooth.1 = (f32[2,104,2560]{2,1,0:T(8,128)}, s32[2,136,128]{2,1,0:T(8,128)}, s32[16,128]{1,0:T(8,128)}) custom-call(f32[4000,128]{1,0:T(8,128)} %bitcast.39, f32[2,100]{1,0:T(2,128)} %decay_ref.3, f32[2,100]{1,0:T(2,128)} %gain_ref.3, f32[2,100]{1,0:T(2,128)} %norm_ref.1, s32[256,128]{1,0:T(8,128)} %bitcast.42, s32[256,128]{1,0:T(8,128)} %bitcast.43, ...), custom_call_target="tpu_custom_call" | custom-call | tf_op jit(solution)/shard_map/smooth/pallas_call | solution.py:644
  54.5 12.9 %count.1.dense_hbm = f32[20,512,256]{2,1,0:T(8,128)} custom-call(s32[2,136,128]{2,1,0:T(8,128)} %get-tuple-element.8.order_ref, s32[16,128]{1,0:T(8,128)} %get-tuple-element.9.edge_ref), custom_call_target="tpu_custom_call" | custom-call | tf_op jit(solution)/shard_map/count/pallas_call | solution.py:604
  67.4 79.0 %adjoint.1 = (f32[4160,128]{1,0:T(8,128)}, f32[208,128]{1,0:T(8,128)}) custom-call(f32[2,104,2560]{2,1,0:T(8,128)} %get-tuple-element.7.t_hbm, f32[20,512,256]{2,1,0:T(8,128)} %count.1.dense_hbm, bf16[800,128]{1,0:T(8,128)(2,1)} %bitcast.41, f32[2,100]{1,0:T(2,128)} %decay_ref.3, f32[2,100]{1,0:T(2,128)} %gain_ref.3), custom_call_target="tpu_custom_call" | custom-call | tf_op jit(solution)/shard_map/adjoint/pallas_call | solution.py:662
  146.5 0.0 copy-start
  146.5 3.0 %slice.6 = f32[4000,128]{1,0:T(8,128)} slice(f32[4160,128]{1,0:T(8,128)} %get-tuple-element.10), slice={[0:4000], [0:128]} | slice | bytes 4096000 | tf_op jit(solution)/shard_map/slice | solution.py:629
  149.5 0.0 copy-done
  149.5 0.6 slice.7
Async XLA Ops:
  146.5 3.1 %copy-start = (f32[208,128]{1,0:T(8,128)S(1)}, f32[208,128]{1,0:T(8,128)}, u32[]{:S(2)}) copy-start(f32[208,128]{1,0:T(8,128)} %get-tuple-element.11) | copy-start | bytes 319492

commit v4 on v3

--- a/solution.py
+++ b/solution.py
@@ -15,7 +15,9 @@
 WORD_SPAN = 4096
 SPARE = 136
 DEEP = 4
-TOGETHER = 2
+TOGETHER = 5
+SPAN = 2
+ROTATE = 0
 CHUNKS = 2
 M_IN, A1, M_OUT, B0, B1, N_IN, C0, N_OUT, E0, E1, X0, X1, DEV_D, DEV_G, DEV_Q = range(15)
 
@@ -51,9 +53,16 @@
     ]
 
 
-def owner_maps(chips, tiles):
+def owner_maps(chips, tiles, turn):
     if chips == 16 and tiles == 13:
-        return lambda r: r + (r + 3) // 4, lambda c: c - (c + 3) // 5, lambda c: lax.rem(c, 5) != 1
+        def around(c, by):
+            return c // 4 * 4 + lax.rem(c + by, 4)
+
+        def tile_of(c):
+            c = around(c, 4 - turn)
+            return c - (c + 3) // 5
+
+        return lambda r: around(r + (r + 3) // 4, turn), tile_of, lambda c: lax.rem(around(c, 4 - turn), 5) != 1
     return lambda r: r, lambda c: c, lambda c: c < tiles
 
 
@@ -63,9 +72,12 @@
     first = core == 0
     width = half // CHUNKS
     partner = {"tm": 2 * chip + 1 - core}
-    chip_of, tile_of, owns = owner_maps(chips, tiles)
-    is_owner = owns(chip)
-    my_tile = tile_of(chip)
+    chip_of, my_tile, is_owner = [], [], []
+    for ch in range(CHUNKS):
+        to_chip, to_tile, owns = owner_maps(chips, tiles, lax.rem(ROTATE * (2 * core + ch), 4))
+        chip_of.append(to_chip)
+        my_tile.append(to_tile(chip))
+        is_owner.append(owns(chip))
     lane = lax.broadcasted_iota(jnp.int32, (ROWS, LANES), 1)
 
     def rows_of(r):
@@ -127,13 +139,13 @@
         return pltpu.make_async_remote_copy(
             src_ref=cbuf.at[ch, rows_of(r), 0 : span(ch)], dst_ref=rbuf.at[ch, chip, :, 0 : span(ch)],
             send_sem=out_send.at[ch, r], recv_sem=out_recv.at[ch, chip],
-            device_id={"tm": 2 * chip_of(r) + core}, device_id_type=MESH)
+            device_id={"tm": 2 * chip_of[ch](r) + core}, device_id_type=MESH)
 
     for ch in range(CHUNKS):
         swap(ch).wait_recv()
 
         def send_chip(k, _, ch=ch):
-            r = lax.rem(chip + 1 + k, tiles)
+            r = lax.rem(my_tile[ch] + 1 + k, tiles)
             (d0, d1), (g0, g1), (q0, q1) = scalars(r)
             f0, f1 = ordered_pair(r, ch, 0, width)
             b0, b1 = ordered_pair(r, ch, width, 2 * width)
@@ -145,7 +157,7 @@
                 cbuf[ch, rows_of(r), 2 * width :] = jnp.where(
                     lane == 0, d0 * d1, jnp.where(lane == 1, g0 * g1, g0 * q1 * d0 + q0))
 
-            @pl.when(chip_of(r) != chip)
+            @pl.when(chip_of[ch](r) != chip)
             def _():
                 out_copy(r, ch).start()
 
@@ -157,14 +169,14 @@
 
     def back_copy(c, ch):
         return pltpu.make_async_remote_copy(
-            src_ref=obuf.at[ch, c], dst_ref=wbuf.at[ch, rows_of(my_tile)],
-            send_sem=back_send.at[ch, c], recv_sem=back_recv.at[ch, my_tile],
+            src_ref=obuf.at[ch, c], dst_ref=wbuf.at[ch, rows_of(my_tile[ch])],
+            send_sem=back_send.at[ch, c], recv_sem=back_recv.at[ch, my_tile[ch]],
             device_id={"tm": 2 * c + core}, device_id_type=MESH)
 
-    @pl.when(is_owner)
-    def _():
-        for ch in range(CHUNKS):
-            rbuf[ch, chip, :, 0 : span(ch)] = cbuf[ch, rows_of(my_tile), 0 : span(ch)]
+    for ch in range(CHUNKS):
+        @pl.when(is_owner[ch])
+        def _(ch=ch):
+            rbuf[ch, chip, :, 0 : span(ch)] = cbuf[ch, rows_of(my_tile[ch]), 0 : span(ch)]
 
             def arrive(k, _, ch=ch):
                 src = lax.rem(chip + k, chips)
@@ -197,7 +209,7 @@
                 return scalar(c, 1) * s + rbuf[ch, c, :, width : 2 * width] + scalar(c, 2) * f
 
             lax.fori_loop(0, chips, homeward, jnp.zeros((ROWS, width), jnp.float32))
-            wbuf[ch, rows_of(my_tile), :] = obuf[ch, chip]
+            wbuf[ch, rows_of(my_tile[ch]), :] = obuf[ch, chip]
 
     def give_copy(r, ch):
         return pltpu.make_async_remote_copy(
@@ -211,14 +223,14 @@
         finish(1, r, side, ch, q1)
         finish(0, r, side, ch, col(r, C0) * q1 + col(r, E0) * p0)
 
-    def turn(k):
-        return lax.rem(my_tile + tiles - k, tiles)
+    def turn(k, ch):
+        return lax.rem(my_tile[ch] + tiles - k, tiles)
 
     for ch in range(CHUNKS):
         def own_half(k, _, ch=ch):
-            r = turn(k)
-
-            @pl.when(chip_of(r) != chip)
+            r = turn(k, ch)
+
+            @pl.when(chip_of[ch](r) != chip)
             def _():
                 pltpu.make_async_remote_copy(
                     src_ref=obuf.at[ch, 0], dst_ref=wbuf.at[ch, rows_of(r)], send_sem=back_send.at[ch, 0],
@@ -238,7 +250,7 @@
         lax.fori_loop(0, tiles, own_half, 0)
 
         def other_half(k, _, ch=ch):
-            r = turn(k)
+            r = turn(k, ch)
             give_copy(r, ch).wait_recv()
             resolve(r, 1 - core, ch, grecv[ch, rows_of(r), 0:width], grecv[ch, rows_of(r), width : 2 * width])
             return 0
@@ -251,7 +263,7 @@
         def drain(r, _, ch=ch):
             give_copy(r, ch).wait_send()
 
-            @pl.when(chip_of(r) != chip)
+            @pl.when(chip_of[ch](r) != chip)
             def _():
                 out_copy(r, ch).wait_send()
 
@@ -259,7 +271,7 @@
 
         lax.fori_loop(0, tiles, drain, 0)
 
-        @pl.when(is_owner)
+        @pl.when(is_owner[ch])
         def _(ch=ch):
             def drain_back(k, _):
                 back_copy(lax.rem(chip + k, chips), ch).wait_send()
@@ -361,7 +373,7 @@
     neighbour = lambda k: {"word": lax.rem(share + 1 + k, shares)}
     meet = greet(chain_peers(chips, chip, core) + [(shares - 1, neighbour)])
     expect(t_hbm, dense_hbm, w_ref, es, ts, tot_ref, sums_ref, load_sem, dense, dense_sem,
-           wraw, w32, wb, wt, tr, ratio, sums, tots)
+           wraw, w32, wb, wt, tr, ratio, sums, tots, table)
     decay = [decay_ref[s : s + 1, :] for s in range(2)]
     gain = [gain_ref[s : s + 1, :] for s in range(2)]
     keep = keep_rows(gain_ref, slices * 2 * chips)
@@ -384,13 +396,13 @@
 
     for k in range(shares - 1):
         tot_copy(k).start()
-    for k in range(shares - 1):
-        sum_copy(k).start()
     total = tot_ref[...]
     for k in range(shares - 1):
         tot_copy(shares - 2 - k).wait_recv()
         total = total + tot_in[k]
-    totals[...] = total
+    table[...] = jnp.zeros_like(table)
+    table[0:ROWS, :] = total
+    totals[...] = table[...].T
 
     def source(s, r, side, ch):
         rows, lanes = pl.ds(pl.multiple_of(r * ROWS, ROWS), ROWS), lanes_of(side, ch, half)
@@ -405,6 +417,10 @@
             out_ref[pl.ds(at + i * slices, ROWS, stride=pitch), :] = grad[:, i * LANES : (i + 1) * LANES]
 
     def gather_sums():
+        for k in range(shares - 1):
+            sum_copy(k).start()
+
+    def take_sums():
         for s in range(slices):
             sums = sums_ref[share, s]
             for k in range(shares - 1):
@@ -414,6 +430,7 @@
             own_ref[pl.ds(s, full, stride=slices), :] = sums
 
     two_sided(chips, chip, core, half, tiles, spread, source, finish, gather_sums, None, bufs)
+    take_sums()
     for k in range(shares - 1):
         tot_copy(k).wait_send()
         sum_copy(k).wait_send()
@@ -535,7 +552,7 @@
 
 
 def expect(t_hbm, dense_hbm, w_ref, es, ts, tot, sums_out, load_sem, dense, dense_sem,
-           wraw, w32, wb, wt, tr, ratio, sums, tots):
+           wraw, w32, wb, wt, tr, ratio, sums, tots, turned):
     slices, full, words = ts.shape
     shares, docs = sums_out.shape[0], w32.shape[1]
     tiles, blocks = words // TILE_W, docs // TILE_D
@@ -544,18 +561,22 @@
         return pltpu.make_async_copy(t_hbm.at[s], ts.at[s], load_sem.at[s])
 
     def fetch(t):
-        slot = lax.rem(t, 2)
-        return pltpu.make_async_copy(dense_hbm.at[t], dense.at[slot], dense_sem.at[slot])
+        return pltpu.make_async_copy(dense_hbm.at[t], dense.at[t], dense_sem.at[t])
 
     for s in range(slices):
         load(s).start()
-    fetch(0).start()
+
+        def ask(j, _, s=s):
+            fetch(s * tiles + j).start()
+            return 0
+
+        lax.fori_loop(0, tiles, ask, 0)
     wraw[w_ref.shape[0] :, :] = jnp.zeros((wraw.shape[0] - w_ref.shape[0], LANES), jnp.float32)
     wraw[0 : w_ref.shape[0], :] = w_ref[...].astype(jnp.float32)
     w32[...] = jnp.zeros_like(w32)
     tr[full // 16 * 16 :, :] = jnp.zeros((128 - full // 16 * 16, words), jnp.bfloat16)
-    lane = lax.broadcasted_iota(jnp.int32, tot.shape, 1)
-    tot[...] = jnp.zeros_like(tot)
+    lane = lax.broadcasted_iota(jnp.int32, (full, LANES), 1)
+    turned[...] = jnp.zeros_like(turned)
 
     for s in range(slices):
         fill_slice(s, wraw, w32, wb, wt)
@@ -565,32 +586,31 @@
         tots[...] = jnp.zeros_like(tots)
 
         def one_tile(j, _, s=s):
-            lanes = pl.ds(pl.multiple_of(j * TILE_W, TILE_W), TILE_W)
+            lanes = pl.ds(pl.multiple_of(j * SPAN * TILE_W, TILE_W), SPAN * TILE_W)
             topic = tr[:, lanes]
-            t = s * tiles + j
-            fetch(t).wait()
-
-            @pl.when(t + 1 < slices * tiles)
-            def _():
-                fetch(t + 1).start()
-
-            for h in range(blocks):
-                rows = slice(h * TILE_D, (h + 1) * TILE_D)
-                mixture = jnp.dot(wt[rows, :], topic, preferred_element_type=jnp.float32)
-                ratio[rows, :] = (dense[lax.rem(t, 2), rows, :] / mixture).astype(jnp.bfloat16)
+            for n in range(SPAN):
+                t = s * tiles + j * SPAN + n
+                part = slice(n * TILE_W, (n + 1) * TILE_W)
+                fetch(t).wait()
+                for h in range(blocks):
+                    rows = slice(h * TILE_D, (h + 1) * TILE_D)
+                    mixture = jnp.dot(wt[rows, :], topic[:, part], preferred_element_type=jnp.float32)
+                    ratio[rows, part] = (dense[t, rows, :] / mixture).astype(jnp.bfloat16)
             sums[...] += lax.dot_general(
                 topic, ratio[...], (((1,), (1,)), ((), ())), preferred_element_type=jnp.float32)
             weighted = jnp.dot(wb[...], ratio[...], preferred_element_type=jnp.float32)
             expected = topic[0:full].astype(jnp.float32) * weighted[0:full]
             es[s, :, lanes] = expected
-            tots[...] += expected
-            return 0
-
-        lax.fori_loop(0, tiles, one_tile, 0)
+            for n in range(SPAN):
+                tots[...] += expected[:, n * TILE_W : (n + 1) * TILE_W]
+            return 0
+
+        lax.fori_loop(0, tiles // SPAN, one_tile, 0)
         for y in range(shares):
             own = slice(y * (docs // shares), (y + 1) * (docs // shares))
             sums_out[y, s] = sums[0:full, own] * w32[0:full, own]
-        tot[...] = jnp.where(lane == s, jnp.sum(tots[...], axis=1, keepdims=True), tot[...])
+        turned[0:full, :] = jnp.where(lane == s, jnp.sum(tots[...], axis=1, keepdims=True), turned[0:full, :])
+    tot[...] = turned[...].T[0:ROWS, :]
 
 
 VMEM_SPEC = pl.BlockSpec(memory_space=pltpu.VMEM)
@@ -669,12 +689,12 @@
             out_specs=(VMEM_SPEC, VMEM_SPEC),
             scratch_shapes=[
                 pltpu.VMEM((slices, full, words), f32), pltpu.VMEM((slices, full, words), f32),
-                pltpu.VMEM((full, LANES), f32), pltpu.VMEM((shares, slices, full, docs // shares), f32),
-                dma((slices,)), pltpu.VMEM((2, docs, TILE_W), f32), dma((2,)),
+                pltpu.VMEM((ROWS, LANES), f32), pltpu.VMEM((shares, slices, full, docs // shares), f32),
+                dma((slices,)), pltpu.VMEM(dense.shape, f32), dma((dense.shape[0],)),
                 pltpu.VMEM((full * slices * docs // LANES, LANES), f32), pltpu.VMEM((128, docs), f32),
                 pltpu.VMEM((128, docs), bf16), pltpu.VMEM((docs, 128), bf16), pltpu.VMEM((128, words), bf16),
-                pltpu.VMEM((docs, TILE_W), bf16), pltpu.VMEM((128, docs), f32), pltpu.VMEM((full, TILE_W), f32),
-                pltpu.VMEM((full, LANES), f32), pltpu.VMEM((shares - 1, full, LANES), f32),
+                pltpu.VMEM((docs, SPAN * TILE_W), bf16), pltpu.VMEM((128, docs), f32), pltpu.VMEM((full, TILE_W), f32),
+                pltpu.VMEM((LANES, LANES), f32), pltpu.VMEM((shares - 1, ROWS, LANES), f32),
                 pltpu.VMEM((shares - 1, slices, full, docs // shares), f32),
                 dma((2, shares - 1)), dma((2, shares - 1)),
             ] + chain_scratch(chips, half, tiles),

time: 151 us -> 136 us (0.901)
  Pallas kernels: 146 us -> 132 us
    pallas_call x1, Pallas kernels: 79 us -> 66.2 us  [local(): pl.pallas_call(functools.partial(adjoint_kernel, chips, shares), out_shap...]
    pallas_call x1, Pallas kernels: 12.9 us -> 11.3 us  [count_entries(): pl.pallas_call(functools.partial(count_kernel, words), out_shape=jax.Shap...]
where the time goes in v4:
time: 136 us
  Pallas kernels  132 us (97%)
  local copies, waits for them, and re-layouts  3.69 us (3%)
    pallas_call x1, Pallas kernels, local(): pl.pallas_call(functools.partial(adjoint_kernel, chips, shares), out_shap...  66.2 us
    pallas_call x1, Pallas kernels, local(): pl.pallas_call(functools.partial(smooth_kernel, chips), out_shape=(jax.Sh...  54.1 us
    pallas_call x1, Pallas kernels, count_entries(): pl.pallas_call(functools.partial(count_kernel, words), out_shape=jax.Shap...  11.3 us
    slice x2, local copies, waits for them, and re-layouts, separated(): x[:rows * columns // LANES * slices]  3.69 us

profile of v4, /device:TPU:1, one launch (start us, length us, event | category | flops | bytes accessed | tf_op | source)
XLA Modules:
  0.0 135.9 jit_solution(17082002143711309841)
XLA Ops:
  0.6 54.1 %smooth.1 = (f32[2,104,2560]{2,1,0:T(8,128)}, s32[2,136,128]{2,1,0:T(8,128)}, s32[16,128]{1,0:T(8,128)}) custom-call(f32[4000,128]{1,0:T(8,128)} %bitcast.39, f32[2,100]{1,0:T(2,128)} %decay_ref.3, f32[2,100]{1,0:T(2,128)} %gain_ref.3, f32[2,100]{1,0:T(2,128)} %norm_ref.1, s32[256,128]{1,0:T(8,128)} %bitcast.42, s32[256,128]{1,0:T(8,128)} %bitcast.43, ...), custom_call_target="tpu_custom_call" | custom-call | tf_op jit(solution)/shard_map/smooth/pallas_call | solution.py:664
  54.7 11.3 %count.1.dense_hbm = f32[20,512,256]{2,1,0:T(8,128)} custom-call(s32[2,136,128]{2,1,0:T(8,128)} %get-tuple-element.8.order_ref, s32[16,128]{1,0:T(8,128)} %get-tuple-element.9.edge_ref), custom_call_target="tpu_custom_call" | custom-call | tf_op jit(solution)/shard_map/count/pallas_call | solution.py:624
  66.0 66.2 %adjoint.1 = (f32[4160,128]{1,0:T(8,128)}, f32[208,128]{1,0:T(8,128)}) custom-call(f32[2,104,2560]{2,1,0:T(8,128)} %get-tuple-element.7.t_hbm, f32[20,512,256]{2,1,0:T(8,128)} %count.1.dense_hbm, bf16[800,128]{1,0:T(8,128)(2,1)} %bitcast.41, f32[2,100]{1,0:T(2,128)} %decay_ref.3, f32[2,100]{1,0:T(2,128)} %gain_ref.3), custom_call_target="tpu_custom_call" | custom-call | tf_op jit(solution)/shard_map/adjoint/pallas_call | solution.py:682
  132.2 0.0 copy-start
  132.3 3.0 %slice.6 = f32[4000,128]{1,0:T(8,128)} slice(f32[4160,128]{1,0:T(8,128)} %get-tuple-element.10), slice={[0:4000], [0:128]} | slice | bytes 4096000 | tf_op jit(solution)/shard_map/slice | solution.py:649
  135.3 0.0 copy-done
  135.3 0.6 slice.7
Async XLA Ops:
  132.2 3.1 %copy-start = (f32[208,128]{1,0:T(8,128)S(1)}, f32[208,128]{1,0:T(8,128)}, u32[]{:S(2)}) copy-start(f32[208,128]{1,0:T(8,128)} %get-tuple-element.11) | copy-start | bytes 319492

commit v5 on v4

--- a/solution.py
+++ b/solution.py
@@ -202,13 +202,15 @@
                 f = obuf[ch, c, :, 0:width]
                 obuf[ch, c, :, width : 2 * width] = s
 
-                @pl.when(c != chip)
-                def _():
-                    back_copy(c, ch).start()
-
                 return scalar(c, 1) * s + rbuf[ch, c, :, width : 2 * width] + scalar(c, 2) * f
 
             lax.fori_loop(0, chips, homeward, jnp.zeros((ROWS, width), jnp.float32))
+
+            def send_back(k, _, ch=ch):
+                back_copy(lax.rem(chip + k, chips), ch).start()
+                return 0
+
+            lax.fori_loop(1, chips, send_back, 0)
             wbuf[ch, rows_of(my_tile[ch]), :] = obuf[ch, chip]
 
     def give_copy(r, ch):
@@ -244,10 +246,17 @@
             gsend[ch, rows_of(r), 0:width] = jnp.where(first, f_mid, f)
             gsend[ch, rows_of(r), width : 2 * width] = jnp.where(first, s, s_mid)
             give_copy(r, ch).start()
-            resolve(r, core, ch, jnp.where(first, f, f_mid), jnp.where(first, s_mid, s))
+            wbuf[ch, rows_of(r), 0:width] = jnp.where(first, f, f_mid)
+            wbuf[ch, rows_of(r), width : 2 * width] = jnp.where(first, s_mid, s)
             return 0
 
         lax.fori_loop(0, tiles, own_half, 0)
+
+        def settle(r, _, ch=ch):
+            resolve(r, core, ch, wbuf[ch, rows_of(r), 0:width], wbuf[ch, rows_of(r), width : 2 * width])
+            return 0
+
+        lax.fori_loop(0, tiles, settle, 0)
 
         def other_half(k, _, ch=ch):
             r = turn(k, ch)

time: 136 us -> 128 us (0.941)
  Pallas kernels: 132 us -> 123 us
    pallas_call x1, Pallas kernels: 66.2 us -> 59.8 us  [local(): pl.pallas_call(functools.partial(adjoint_kernel, chips, shares), out_shap...]
    pallas_call x1, Pallas kernels: 54.1 us -> 51.7 us  [local(): pl.pallas_call(functools.partial(smooth_kernel, chips), out_shape=(jax.Sh...]
where the time goes in v5:
time: 128 us; the launch traced here: 127 us
  Pallas kernels  123 us (96%)
  local copies, waits for them, and re-layouts  3.69 us (3%)
    pallas_call x1, Pallas kernels, local(): pl.pallas_call(functools.partial(adjoint_kernel, chips, shares), out_shap...  59.8 us
    pallas_call x1, Pallas kernels, local(): pl.pallas_call(functools.partial(smooth_kernel, chips), out_shape=(jax.Sh...  51.7 us
    pallas_call x1, Pallas kernels, count_entries(): pl.pallas_call(functools.partial(count_kernel, words), out_shape=jax.Shap...  11.3 us
    slice x2, local copies, waits for them, and re-layouts, separated(): x[:rows * columns // LANES * slices]  3.69 us

profile of v5, /device:TPU:1, one launch (start us, length us, event | category | flops | bytes accessed | tf_op | source)
XLA Modules:
  0.0 127.2 jit_solution(17835737479917364678)
XLA Ops:
  0.6 51.7 %smooth.1 = (f32[2,104,2560]{2,1,0:T(8,128)}, s32[2,136,128]{2,1,0:T(8,128)}, s32[16,128]{1,0:T(8,128)}) custom-call(f32[4000,128]{1,0:T(8,128)} %bitcast.39, f32[2,100]{1,0:T(2,128)} %decay_ref.3, f32[2,100]{1,0:T(2,128)} %gain_ref.3, f32[2,100]{1,0:T(2,128)} %norm_ref.1, s32[256,128]{1,0:T(8,128)} %bitcast.42, s32[256,128]{1,0:T(8,128)} %bitcast.43, ...), custom_call_target="tpu_custom_call" | custom-call | tf_op jit(solution)/shard_map/smooth/pallas_call | solution.py:673
  52.4 11.3 %count.1.dense_hbm = f32[20,512,256]{2,1,0:T(8,128)} custom-call(s32[2,136,128]{2,1,0:T(8,128)} %get-tuple-element.8.order_ref, s32[16,128]{1,0:T(8,128)} %get-tuple-element.9.edge_ref), custom_call_target="tpu_custom_call" | custom-call | tf_op jit(solution)/shard_map/count/pallas_call | solution.py:633
  63.7 59.8 %adjoint.1 = (f32[4160,128]{1,0:T(8,128)}, f32[208,128]{1,0:T(8,128)}) custom-call(f32[2,104,2560]{2,1,0:T(8,128)} %get-tuple-element.7.t_hbm, f32[20,512,256]{2,1,0:T(8,128)} %count.1.dense_hbm, bf16[800,128]{1,0:T(8,128)(2,1)} %bitcast.41, f32[2,100]{1,0:T(2,128)} %decay_ref.3, f32[2,100]{1,0:T(2,128)} %gain_ref.3), custom_call_target="tpu_custom_call" | custom-call | tf_op jit(solution)/shard_map/adjoint/pallas_call | solution.py:691
  123.5 0.0 copy-start
  123.5 3.0 %slice.6 = f32[4000,128]{1,0:T(8,128)} slice(f32[4160,128]{1,0:T(8,128)} %get-tuple-element.10), slice={[0:4000], [0:128]} | slice | bytes 4096000 | tf_op jit(solution)/shard_map/slice | solution.py:658
  126.5 0.0 copy-done
  126.5 0.6 slice.7
Async XLA Ops:
  123.5 3.1 %copy-start = (f32[208,128]{1,0:T(8,128)S(1)}, f32[208,128]{1,0:T(8,128)}, u32[]{:S(2)}) copy-start(f32[208,128]{1,0:T(8,128)} %get-tuple-element.11) | copy-start | bytes 319492

commit v6 on v5

--- a/solution.py
+++ b/solution.py
@@ -14,7 +14,7 @@
 TILE_D = 256
 WORD_SPAN = 4096
 SPARE = 136
-DEEP = 4
+DEEP = 8
 TOGETHER = 5
 SPAN = 2
 ROTATE = 0

time: 128 us -> 128 us (level)
  no operation moved by 1% of the time
where the time goes in v6:
time: 128 us; the launch traced here: 127 us
  Pallas kernels  122 us (95%)
  local copies, waits for them, and re-layouts  3.69 us (3%)
    pallas_call x1, Pallas kernels, local(): pl.pallas_call(functools.partial(adjoint_kernel, chips, shares), out_shap...  60.4 us
    pallas_call x1, Pallas kernels, local(): pl.pallas_call(functools.partial(smooth_kernel, chips), out_shape=(jax.Sh...  51.7 us
    pallas_call x1, Pallas kernels, count_entries(): pl.pallas_call(functools.partial(count_kernel, words), out_shape=jax.Shap...  10.2 us
    slice x2, local copies, waits for them, and re-layouts, separated(): x[:rows * columns // LANES * slices]  3.69 us

profile of v6, /device:TPU:1, one launch (start us, length us, event | category | flops | bytes accessed | tf_op | source)
XLA Modules:
  0.0 126.7 jit_solution(1372407705637692377)
XLA Ops:
  0.6 51.7 %smooth.1 = (f32[2,104,2560]{2,1,0:T(8,128)}, s32[2,136,128]{2,1,0:T(8,128)}, s32[16,128]{1,0:T(8,128)}) custom-call(f32[4000,128]{1,0:T(8,128)} %bitcast.39, f32[2,100]{1,0:T(2,128)} %decay_ref.3, f32[2,100]{1,0:T(2,128)} %gain_ref.3, f32[2,100]{1,0:T(2,128)} %norm_ref.1, s32[256,128]{1,0:T(8,128)} %bitcast.42, s32[256,128]{1,0:T(8,128)} %bitcast.43, ...), custom_call_target="tpu_custom_call" | custom-call | tf_op jit(solution)/shard_map/smooth/pallas_call | solution.py:673
  52.4 10.2 %count.1.dense_hbm = f32[20,512,256]{2,1,0:T(8,128)} custom-call(s32[2,136,128]{2,1,0:T(8,128)} %get-tuple-element.8.order_ref, s32[16,128]{1,0:T(8,128)} %get-tuple-element.9.edge_ref), custom_call_target="tpu_custom_call" | custom-call | tf_op jit(solution)/shard_map/count/pallas_call | solution.py:633
  62.6 60.4 %adjoint.1 = (f32[4160,128]{1,0:T(8,128)}, f32[208,128]{1,0:T(8,128)}) custom-call(f32[2,104,2560]{2,1,0:T(8,128)} %get-tuple-element.7.t_hbm, f32[20,512,256]{2,1,0:T(8,128)} %count.1.dense_hbm, bf16[800,128]{1,0:T(8,128)(2,1)} %bitcast.41, f32[2,100]{1,0:T(2,128)} %decay_ref.3, f32[2,100]{1,0:T(2,128)} %gain_ref.3), custom_call_target="tpu_custom_call" | custom-call | tf_op jit(solution)/shard_map/adjoint/pallas_call | solution.py:691
  123.0 0.0 copy-start
  123.0 3.0 %slice.6 = f32[4000,128]{1,0:T(8,128)} slice(f32[4160,128]{1,0:T(8,128)} %get-tuple-element.10), slice={[0:4000], [0:128]} | slice | bytes 4096000 | tf_op jit(solution)/shard_map/slice | solution.py:658
  126.0 0.0 copy-done
  126.0 0.6 slice.7
Async XLA Ops:
  123.0 3.1 %copy-start = (f32[208,128]{1,0:T(8,128)S(1)}, f32[208,128]{1,0:T(8,128)}, u32[]{:S(2)}) copy-start(f32[208,128]{1,0:T(8,128)} %get-tuple-element.11) | copy-start | bytes 319492
